TPU v7x, 128 devices: a whole 4x4x4 slice. The times are simulated.
128 devices in a mesh: chan: 16 (over y_lo, x, core), row: 8 (over y_hi, z).
Axes of the slice: x: 4, y: 4 (y_hi: 2, y_lo: 2; y = y_hi * 2 + y_lo), z: 4, core: 2. Of those that a mesh axis runs over, the one named last changes fastest.
Arguments:
- samples: bfloat16 [8, 128, 65536], P(None, 'chan', 'row'), may hold values from -6 to 6
- history: bfloat16 [8, 128, 7168], P(None, 'chan'), may hold values from -6 to 6
- antenna_flags: int32 [1024], replicated, may hold values 0 or 1
- beam_delays: int32 [256, 1024], replicated, may hold values from 0 to 1023
Outputs:
- visibilities: bfloat16 [512, 2, 1024, 1024], P('chan', None, 'row')
- beam_series: float32 [256, 64, 1024], P(('chan', 'row'))
All inputs are finite; a program needn't handle non-finite values.
Results may differ from a plain program's by a relative error of at most 0.0075.
Values may be sent and summed in bfloat16 or wider, within the bound.
A program may use at most 128 MiB of HBM per device.

v0:
```python
import math

import jax
import jax.numpy as jnp
import numpy as np
from jax import lax
from jax.experimental import pallas as pl
from jax.experimental.pallas import tpu as pltpu
from jax.sharding import PartitionSpec as P

A = 1024
FL = 1024
NCH = 512
TAPS = 8
BEAMS = 256
NC = 16
NR = 8
CHB = NCH // NC
ROWS = A // NR
AL = ROWS // NC
F = 64
Q = 4
CH = CHB // Q
KK = NC * CH
HALF = CH // 2
HIST = (TAPS - 1) * FL
SPAN = (F // NR) * FL
MESH = pl.DeviceIdType.MESH
F32 = jnp.float32
BF16 = jnp.bfloat16
NKIND = 16


def tap_table():
    position = (np.arange(TAPS * FL, dtype=np.int32).astype(np.float32) + np.float32(0.5)).astype(np.float64)
    centred = position / FL - TAPS / 2.0
    window = 0.5 - 0.5 * np.cos(2.0 * math.pi * position / (TAPS * FL))
    return (np.sinc(centred) * window).reshape(TAPS, FL).astype(np.float32)


def cos_sin(m):
    quarter = lax.shift_right_logical(m, 8)
    x = ((m & 255) - 128).astype(F32) * (2.0 * math.pi / FL)
    x2 = x * x
    s = x * (1.0 + x2 * (-1.0 / 6 + x2 * (1.0 / 120 + x2 * (-1.0 / 5040 + x2 * (1.0 / 362880)))))
    c = 1.0 + x2 * (-0.5 + x2 * (1.0 / 24 + x2 * (-1.0 / 720 + x2 * (1.0 / 40320 + x2 * (-1.0 / 3628800)))))
    root = math.sqrt(0.5)
    ca = (c - s) * root
    sa = (c + s) * root
    odd = (quarter & 1) == 1
    neg = quarter >= 2
    cv = jnp.where(odd, -sa, ca)
    sv = jnp.where(odd, ca, sa)
    return jnp.where(neg, -cv, cv), jnp.where(neg, -sv, sv)


def nt(lhs, rhs):
    return lax.dot_general(lhs, rhs, (((1,), (1,)), ((), ())), preferred_element_type=F32)


def front_kernel(
    samples, history, taps, flags, delays, g_out, series,
    ext, filt32, filt, dftc, dfts, tmp, sbuf, abuf, g, transit, wcos, wall, bs, bsend, z_in, ptab, qtab,
    s_row, r_row, s_loc, s_ch, r_ch, s_g, r_g, s_bm, r_bm, s_out,
):
    c = lax.axis_index("chan")
    r = lax.axis_index("row")
    c_low = lax.rem(c, 8)
    y_lo = c // 8
    h = r // 4
    z = lax.rem(r, 4)
    y = 2 * h + y_lo
    zp = lax.rem(z + 1, 4)
    zm = lax.rem(z + 3, 4)
    z2 = lax.rem(z + 2, 4)
    yp = lax.rem(y + 1, 4)
    ym = lax.rem(y + 3, 4)
    up = {"chan": c, "row": h * 4 + zp}
    dn = {"chan": c, "row": h * 4 + zm}
    fw = {"chan": lax.rem(yp, 2) * 8 + c_low, "row": (yp // 2) * 4 + z}
    bw = {"chan": lax.rem(ym, 2) * 8 + c_low, "row": (ym // 2) * 4 + z}

    def remote(src, dst, ss, rs, dev):
        return pltpu.make_async_remote_copy(
            src_ref=src, dst_ref=dst, send_sem=ss, recv_sem=rs, device_id=dev, device_id_type=MESH
        )

    barrier = pltpu.get_barrier_semaphore()
    for d in range(1, NR):
        pl.semaphore_signal(barrier, inc=1, device_id={"chan": c, "row": lax.rem(r + d, NR)}, device_id_type=MESH)
    for d in range(1, NC):
        pl.semaphore_signal(barrier, inc=1, device_id={"chan": lax.rem(c + d, NC), "row": r}, device_id_type=MESH)
    pl.semaphore_signal(barrier, inc=1, device_id=fw, device_id_type=MESH)
    pl.semaphore_signal(barrier, inc=1, device_id=bw, device_id_type=MESH)
    pl.semaphore_wait(barrier, NR - 1 + NC - 1 + 2)

    def span(row):
        return ext.at[:, pl.ds(pl.multiple_of(HIST + row * SPAN, FL), SPAN)]

    row_sends = []
    for d in range(1, NR):
        to = lax.rem(r + d, NR)
        cp = remote(samples.at[to], span(r), s_row.at[d], r_row.at[d], {"chan": c, "row": to})
        cp.start()
        row_sends.append(cp)
    own = pltpu.make_async_copy(samples.at[r], span(r), s_loc.at[0])
    own.start()
    hist = pltpu.make_async_copy(history.at[r], ext.at[:, pl.ds(0, HIST)], s_loc.at[1])
    hist.start()

    def dft_rows(i, _):
        row = i * 16 + lax.broadcasted_iota(jnp.int32, (16, FL), 0)
        q, rest = row // KK, row % KK
        k = (rest // CH) * CHB + q * CH + rest % CH
        n = lax.broadcasted_iota(jnp.int32, (16, FL), 1)
        cv, sv = cos_sin((k * n) & (FL - 1))
        scale = 1.0 / math.sqrt(FL)
        at = pl.ds(pl.multiple_of(i * 16, 16), 16)
        dftc[at, :] = (cv * scale).astype(BF16)
        dfts[at, :] = (-sv * scale).astype(BF16)
        return 0

    lax.fori_loop(0, NCH // 16, dft_rows, 0)

    def synth_rows(i, _):
        k = i * 16 + lax.broadcasted_iota(jnp.int32, (16, FL), 0)
        n = lax.broadcasted_iota(jnp.int32, (16, FL), 1)
        cv, sv = cos_sin((k * n) & (FL - 1))
        scale = 1.0 / math.sqrt(NCH)
        at = pl.ds(pl.multiple_of(i * 16, 16), 16)
        ptab[at, :] = (cv * scale).astype(BF16)
        qtab[at, :] = (-sv * scale).astype(BF16)
        return 0

    lax.fori_loop(0, NCH // 16, synth_rows, 0)

    for e in range(2):
        for i in range(NC):
            wcos[e * NC + i : e * NC + i + 1, :] = delays[pl.ds(i * 2 * NR + 2 * r + e, 1), :]

    def steer(i, _):
        lanes = pl.ds(pl.multiple_of(i * 128, 128), 128)
        d = wcos[:, lanes]
        cr, ci = cos_sin((d * (c * CHB)) & (FL - 1))
        sr, si = cos_sin(d)
        scale = 1.0 / math.sqrt(A)
        for ch in range(CHB):
            wall[ch, 0:32, lanes] = (cr * scale).astype(BF16)
            wall[ch, 32:64, lanes] = (-ci * scale).astype(BF16)
            cr, ci = cr * sr - ci * si, cr * si + ci * sr
        return 0

    lax.fori_loop(0, A // 128, steer, 0)

    own.wait()
    hist.wait()
    for d in range(1, NR):
        frm = lax.rem(r + NR - d, NR)
        remote(samples.at[frm], span(frm), s_row.at[d], r_row.at[d], {"chan": c, "row": frm}).wait_recv()

    def pfb(i, _):
        lanes = pl.ds(pl.multiple_of(i * 128, 128), 128)
        tap = [jnp.broadcast_to(taps[t : t + 1, lanes], (AL, 128)) for t in range(TAPS)]
        win = [ext[:, pl.ds(pl.multiple_of(t * FL + i * 128, 128), 128)].astype(F32) for t in range(TAPS - 1)]
        for f in range(F):
            win.append(ext[:, pl.ds(pl.multiple_of((f + TAPS - 1) * FL + i * 128, 128), 128)].astype(F32))
            acc = win[f] * tap[0]
            for t in range(1, TAPS):
                acc = acc + win[f + t] * tap[t]
            filt32[f * AL : (f + 1) * AL, :] = acc
        for a in range(AL):
            for b in range(F // 16):
                filt[a * F + b * 16 : a * F + (b + 1) * 16, lanes] = filt32[
                    pl.ds(b * 16 * AL + a, 16, stride=AL), :
                ].astype(BF16)
        return 0

    lax.fori_loop(0, FL // 128, pfb, 0)

    low = lax.broadcasted_iota(jnp.int32, (KK, 128), 1) < 64
    for q in range(Q):
        rows = slice(q * KK, (q + 1) * KK)
        re = nt(dftc[rows, :], filt[...])
        im = nt(dfts[rows, :], filt[...])
        for t in range(AL // 2):
            rt = re[:, t * 128 : (t + 1) * 128]
            it = im[:, t * 128 : (t + 1) * 128]
            tmp[(2 * t) * KK : (2 * t + 1) * KK, :] = jnp.where(low, rt, pltpu.roll(it, 64, 1))
            tmp[(2 * t + 1) * KK : (2 * t + 2) * KK, :] = jnp.where(low, pltpu.roll(rt, 64, 1), it)

        def turn(i, _, q=q):
            for p in range(CH // 2):
                pair = [tmp[pl.ds(i * CH + 2 * p + e, AL, stride=KK), :] for e in range(2)]
                sbuf[q, i, p * 16 : (p + 1) * 16, :] = jnp.concatenate(pair, axis=0).astype(BF16)
            return 0

        lax.fori_loop(0, NC, turn, 0)
        for d in range(1, NC):
            to = lax.rem(c + d, NC)
            remote(sbuf.at[q, to], abuf.at[q, c], s_ch.at[q, d], r_ch.at[q, d], {"chan": to, "row": r}).start()
        abuf[q, c] = sbuf[q, c]

    row_own = [h * 4 + v for v in (z, zp, z2, zm)]
    row_oth = [(1 - h) * 4 + v for v in (z, zp, z2, zm)]
    h_bw = ym // 2
    h_fw = yp // 2

    def part(row, q, half=None):
        if half is None:
            return g.at[row, pl.ds(q * CH, CH)]
        return g.at[row, pl.ds(q * CH + half * HALF, HALF)]

    sent = []

    def send(q, kind, src, dst, dev):
        cp = remote(src, dst, s_g.at[q, kind], r_g.at[q, kind], dev)
        cp.start()
        sent.append(cp)

    def arrived(q, kind, dst, dev):
        remote(dst, dst, s_g.at[q, kind], r_g.at[q, kind], dev).wait_recv()

    def phase0(q):
        for d in range(1, NC):
            frm = lax.rem(c + NC - d, NC)
            remote(sbuf.at[q, frm], abuf.at[q, frm], s_ch.at[q, d], r_ch.at[q, d], {"chan": frm, "row": r}).wait_recv()
        fl = flags[pl.ds(pl.multiple_of(r * ROWS, ROWS), ROWS), :]
        for p in range(CH // 2):
            x = abuf[q, :, p * 16 : (p + 1) * 16, :].astype(F32)
            for e in range(2):
                v = x[:, e * AL : (e + 1) * AL, :].reshape(ROWS, 128) * fl
                g[r, q * CH + 2 * p + e] = v.astype(BF16)
        send(q, 0, part(r, q), part(r, q), up)
        send(q, 1, part(r, q), part(r, q), dn)
        send(q, 4, part(r, q, 0), transit.at[0, q], fw)
        send(q, 5, part(r, q, 1), transit.at[1, q], bw)

    def phase1(q):
        arrived(q, 0, part(row_own[3], q), dn)
        send(q, 2, part(row_own[3], q, 0), part(row_own[3], q, 0), up)
        arrived(q, 1, part(row_own[1], q), up)
        send(q, 3, part(row_own[1], q, 1), part(row_own[1], q, 1), dn)
        arrived(q, 4, transit.at[0, q], bw)
        send(q, 6, transit.at[0, q], part(h_bw * 4 + z, q, 0), fw)
        arrived(q, 5, transit.at[1, q], fw)
        send(q, 7, transit.at[1, q], part(h_fw * 4 + z, q, 1), bw)

    def phase2(q):
        arrived(q, 6, part(row_oth[0], q, 0), bw)
        send(q, 8, part(row_oth[0], q, 0), part(row_oth[0], q, 0), up)
        send(q, 10, part(row_oth[0], q, 0), part(row_oth[0], q, 0), dn)
        arrived(q, 7, part(row_oth[0], q, 1), fw)
        send(q, 9, part(row_oth[0], q, 1), part(row_oth[0], q, 1), up)
        send(q, 11, part(row_oth[0], q, 1), part(row_oth[0], q, 1), dn)
        arrived(q, 2, part(row_own[2], q, 0), dn)
        send(q, 12, part(row_own[2], q, 0), transit.at[2, q], fw)
        arrived(q, 3, part(row_own[2], q, 1), up)
        send(q, 13, part(row_own[2], q, 1), transit.at[3, q], bw)

    def phase3(q):
        arrived(q, 12, transit.at[2, q], bw)
        send(q, 14, transit.at[2, q], part(h_bw * 4 + z2, q, 0), fw)
        arrived(q, 13, transit.at[3, q], fw)
        send(q, 15, transit.at[3, q], part(h_fw * 4 + z2, q, 1), bw)

    lane = lax.broadcasted_iota(jnp.int32, (32, 128), 1) < 64
    outs = []

    def phase4(q):
        arrived(q, 8, part(row_oth[3], q, 0), dn)
        arrived(q, 9, part(row_oth[3], q, 1), dn)
        arrived(q, 10, part(row_oth[1], q, 0), up)
        arrived(q, 11, part(row_oth[1], q, 1), up)
        arrived(q, 14, part(row_oth[2], q, 0), bw)
        arrived(q, 15, part(row_oth[2], q, 1), fw)
        cp = pltpu.make_async_copy(
            g.at[:, pl.ds(q * CH, CH)], g_out.at[:, pl.ds(q * CH, CH)], s_out.at[q]
        )
        cp.start()
        outs.append(cp)

        def beams(i, _):
            ch = q * CH + i
            x = g[:, ch].reshape(A, 128)
            acc = jnp.dot(wall[ch], x, preferred_element_type=F32)
            turned = pltpu.roll(acc[32:, :], 64, 1)
            bs[pl.ds(pl.multiple_of(ch * 32, 32), 32), :] = acc[:32, :] + jnp.where(lane, -turned, turned)
            return 0

        lax.fori_loop(0, CH, beams, 0)

    for s in range(Q + 4):
        for k, phase in enumerate((phase0, phase1, phase2, phase3, phase4)):
            if 0 <= s - k < Q:
                phase(s - k)

    def pack(i, _):
        for e in range(2):
            bsend[i, e] = bs[pl.ds(e * 16 + i, CHB, stride=32), :].astype(BF16)
        return 0

    lax.fori_loop(0, NC, pack, 0)
    beam_sends = []
    for d in range(1, NC):
        to = lax.rem(c + d, NC)
        cp = remote(bsend.at[to], z_in.at[c], s_bm.at[d], r_bm.at[d], {"chan": to, "row": r})
        cp.start()
        beam_sends.append(cp)
    z_in[c] = bsend[c]
    for d in range(1, NC):
        frm = lax.rem(c + NC - d, NC)
        remote(bsend.at[frm], z_in.at[frm], s_bm.at[d], r_bm.at[d], {"chan": frm, "row": r}).wait_recv()
    for e in range(2):
        zt = z_in[:, e].reshape(NCH, 128).astype(F32).T.astype(BF16)
        series[e] = jnp.dot(zt[:F, :], ptab[...], preferred_element_type=F32) + jnp.dot(
            zt[F:, :], qtab[...], preferred_element_type=F32
        )

    for cp in row_sends:
        cp.wait_send()
    for q in range(Q):
        for d in range(1, NC):
            to = lax.rem(c + d, NC)
            remote(sbuf.at[q, to], abuf.at[q, c], s_ch.at[q, d], r_ch.at[q, d], {"chan": to, "row": r}).wait_send()
    for cp in sent:
        cp.wait_send()
    for cp in beam_sends:
        cp.wait_send()
    for cp in outs:
        cp.wait()


def front(samples, history, taps, flags, delays):
    vmem = pl.BlockSpec(memory_space=pltpu.VMEM)
    hbm = pl.BlockSpec(memory_space=pl.ANY)
    dma = pltpu.SemaphoreType.DMA
    return pl.pallas_call(
        front_kernel,
        out_shape=(
            jax.ShapeDtypeStruct((NR, CHB, ROWS, 128), BF16),
            jax.ShapeDtypeStruct((2, F, FL), F32),
        ),
        in_specs=[vmem, hbm, vmem, vmem, vmem],
        out_specs=(hbm, vmem),
        scratch_shapes=[
            pltpu.VMEM((AL, HIST + F * FL), BF16),
            pltpu.VMEM((F * AL, 128), F32),
            pltpu.VMEM((F * AL, FL), BF16),
            pltpu.VMEM((NCH, FL), BF16),
            pltpu.VMEM((NCH, FL), BF16),
            pltpu.VMEM((AL * KK, 128), F32),
            pltpu.VMEM((Q, NC, CH * AL, 128), BF16),
            pltpu.VMEM((Q, NC, CH * AL, 128), BF16),
            pltpu.VMEM((NR, CHB, ROWS, 128), BF16),
            pltpu.VMEM((4, Q, HALF, ROWS, 128), BF16),
            pltpu.VMEM((32, A), jnp.int32),
            pltpu.VMEM((CHB, 64, A), BF16),
            pltpu.VMEM((CHB * 32, 128), F32),
            pltpu.VMEM((NC, 2, CHB, 128), BF16),
            pltpu.VMEM((NC, 2, CHB, 128), BF16),
            pltpu.VMEM((NCH, FL), BF16),
            pltpu.VMEM((NCH, FL), BF16),
            dma((NR,)),
            dma((NR,)),
            dma((2,)),
            dma((Q, NC)),
            dma((Q, NC)),
            dma((Q, NKIND)),
            dma((Q, NKIND)),
            dma((NC,)),
            dma((NC,)),
            dma((Q,)),
        ],
        compiler_params=pltpu.CompilerParams(
            collective_id=0, has_side_effects=True, vmem_limit_bytes=58 * 2**20
        ),
        name="front",
    )(samples, history, taps, flags, delays)


CB = 2


def gram_kernel(g, out):
    r = lax.axis_index("row")
    low = lax.broadcasted_iota(jnp.int32, (ROWS, 128), 1) < 64
    for i in range(CB):
        own = g[r, i]
        turned = pltpu.roll(own.astype(F32), 64, 1)
        lhs = jnp.concatenate([own, jnp.where(low, turned, -turned).astype(BF16)], axis=0)
        acc = nt(lhs, g[:, i].reshape(A, 128)) * (1.0 / F)
        out[i, 0] = acc[:ROWS].astype(BF16)
        out[i, 1] = acc[ROWS:].astype(BF16)


def gram(g):
    return pl.pallas_call(
        gram_kernel,
        out_shape=jax.ShapeDtypeStruct((CHB, 2, ROWS, A), BF16),
        grid=(CHB // CB,),
        in_specs=[pl.BlockSpec((NR, CB, ROWS, 128), lambda i: (0, i, 0, 0))],
        out_specs=pl.BlockSpec((CB, 2, ROWS, A), lambda i: (i, 0, 0, 0)),
        name="gram",
    )(g)


def body(samples, history, antenna_flags, beam_delays):
    flags = jnp.broadcast_to(antenna_flags.astype(F32)[:, None], (A, 128))
    g, series = front(samples, history, jnp.asarray(tap_table()), flags, beam_delays)
    return gram(g), series


def solution(mesh):
    in_specs = (P(None, "chan", "row"), P(None, "chan", None), P(), P())
    out_specs = (P("chan", None, "row", None), P(("chan", "row"), None, None))
    return jax.shard_map(body, mesh=mesh, in_specs=in_specs, out_specs=out_specs, check_vma=False)
```

profile of v0, /device:TPU:1, one launch (start us, length us, event | category | flops | bytes accessed | tf_op | source)
XLA Modules:
  0.0 125.7 jit_solution(12192580052859989627)
XLA Ops:
  0.6 0.7 convert_element_type.3
  1.3 1.0 broadcast_in_dim.2.flags
  2.3 106.1 %front.1 = (bf16[8,32,128,128]{3,2,1,0:T(8,128)(2,1)}, f32[2,64,1024]{2,1,0:T(8,128)}) custom-call(bf16[8,8,8192]{2,1,0:T(8,128)(2,1)} %samples.1, bf16[8,8,7168]{2,1,0:T(8,128)(2,1)} %history.1, f32[8,1024]{1,0:T(8,128)} %constant.2.clone.taps, f32[1024,128]{1,0:T(8,128)} %broadcast_in_dim.2.flags, s32[256,1024]{1,0:T(8,128)} %delays.1), custom_call_target="tpu_custom_call" | custom-call | tf_op jit(solution)/shard_map/front/pallas_call | solution.py:337
  108.4 0.0 copy-start
  108.5 16.4 %gram.1 = bf16[32,2,128,1024]{3,2,1,0:T(8,128)(2,1)} custom-call(bf16[8,32,128,128]{3,2,1,0:T(8,128)(2,1)} %get-tuple-element.4.g), custom_call_target="tpu_custom_call" | custom-call | tf_op jit(solution)/shard_map/gram/pallas_call | solution.py:397
  124.9 0.0 copy-done
  124.9 0.8 copy.8
Async XLA Ops:
  108.4 16.5 %copy-start = (f32[2,64,1024]{2,1,0:T(8,128)S(1)}, f32[2,64,1024]{2,1,0:T(8,128)}, u32[]{:S(2)}) copy-start(f32[2,64,1024]{2,1,0:T(8,128)} %get-tuple-element.9) | copy-start | bytes 1572868
where the time goes:
time: 126 us
  Pallas kernels  123 us (98%)
  local copies, waits for them, and re-layouts  1.79 us (1%)
    pallas_call x1, Pallas kernels, front(): pl.pallas_call(front_kernel, out_shape=(jax.ShapeDtypeStruct((NR, CHB, RO...  106 us
    pallas_call x1, Pallas kernels, gram(): pl.pallas_call(gram_kernel, out_shape=jax.ShapeDtypeStruct((CHB, 2, ROWS,...  16.4 us

commit v1 on v0

v1 whole, which is shorter than its diff:
```python
import math

import jax
import jax.numpy as jnp
import numpy as np
from jax import lax
from jax.experimental import pallas as pl
from jax.experimental.pallas import tpu as pltpu
from jax.sharding import PartitionSpec as P

A = 1024
FL = 1024
NCH = 512
TAPS = 8
BEAMS = 256
NC = 16
NR = 8
CHB = NCH // NC
ROWS = A // NR
AL = ROWS // NC
F = 64
Q = 4
CH = CHB // Q
KK = NC * CH
HALF = CH // 2
HIST = (TAPS - 1) * FL
SPAN = (F // NR) * FL
MESH = pl.DeviceIdType.MESH
F32 = jnp.float32
BF16 = jnp.bfloat16
NKIND = 16


def tap_table():
    position = (np.arange(TAPS * FL, dtype=np.int32).astype(np.float32) + np.float32(0.5)).astype(np.float64)
    centred = position / FL - TAPS / 2.0
    window = 0.5 - 0.5 * np.cos(2.0 * math.pi * position / (TAPS * FL))
    return (np.sinc(centred) * window).reshape(TAPS, FL).astype(np.float32)


def cos_sin(m):
    quarter = lax.shift_right_logical(m, 8)
    x = ((m & 255) - 128).astype(F32) * (2.0 * math.pi / FL)
    x2 = x * x
    s = x * (1.0 + x2 * (-1.0 / 6 + x2 * (1.0 / 120 + x2 * (-1.0 / 5040 + x2 * (1.0 / 362880)))))
    c = 1.0 + x2 * (-0.5 + x2 * (1.0 / 24 + x2 * (-1.0 / 720 + x2 * (1.0 / 40320 + x2 * (-1.0 / 3628800)))))
    root = math.sqrt(0.5)
    ca = (c - s) * root
    sa = (c + s) * root
    odd = (quarter & 1) == 1
    neg = quarter >= 2
    cv = jnp.where(odd, -sa, ca)
    sv = jnp.where(odd, ca, sa)
    return jnp.where(neg, -cv, cv), jnp.where(neg, -sv, sv)


def nt(lhs, rhs):
    return lax.dot_general(lhs, rhs, (((1,), (1,)), ((), ())), preferred_element_type=F32)


def gram_lhs(own):
    low = lax.broadcasted_iota(jnp.int32, (ROWS, 128), 1) < 64
    turned = pltpu.roll(own.astype(F32), 64, 1)
    return jnp.concatenate([own, jnp.where(low, turned, -turned).astype(BF16)], axis=0) * BF16(1.0 / F)


def front_kernel(
    samples, history, taps, flags, delays, g, vis, z_in, ptab, qtab,
    ext, hop, filt32, filt, dftc, dfts, tmp, sbuf, abuf, transit, fl, wcos, wall, bs, bsend,
    s_row, r_row, s_hop, r_hop, s_far, r_far, s_loc, s_ch, r_ch, s_g, r_g, s_bm, r_bm,
):
    c = lax.axis_index("chan")
    r = lax.axis_index("row")
    c_low = lax.rem(c, 8)
    y_lo = c // 8
    h = r // 4
    z = lax.rem(r, 4)
    y = 2 * h + y_lo
    zp = lax.rem(z + 1, 4)
    zm = lax.rem(z + 3, 4)
    z2 = lax.rem(z + 2, 4)
    yp = lax.rem(y + 1, 4)
    ym = lax.rem(y + 3, 4)
    h_fw = yp // 2
    h_bw = ym // 2
    c_fw = lax.rem(yp, 2) * 8 + c_low
    c_bw = lax.rem(ym, 2) * 8 + c_low
    up = {"chan": c, "row": h * 4 + zp}
    dn = {"chan": c, "row": h * 4 + zm}
    fw = {"chan": c_fw, "row": h_fw * 4 + z}
    bw = {"chan": c_bw, "row": h_bw * 4 + z}
    fw_up = {"chan": c_fw, "row": h_fw * 4 + zp}
    bw_dn = {"chan": c_bw, "row": h_bw * 4 + zm}
    row_own = [h * 4 + v for v in (z, zp, z2, zm)]
    row_oth = [(1 - h) * 4 + v for v in (z, zp, z2, zm)]

    def remote(src, dst, ss, rs, dev):
        return pltpu.make_async_remote_copy(
            src_ref=src, dst_ref=dst, send_sem=ss, recv_sem=rs, device_id=dev, device_id_type=MESH
        )

    barrier = pltpu.get_barrier_semaphore()
    for d in range(1, NR):
        pl.semaphore_signal(barrier, inc=1, device_id={"chan": c, "row": lax.rem(r + d, NR)}, device_id_type=MESH)
    for d in range(1, NC):
        pl.semaphore_signal(barrier, inc=1, device_id={"chan": lax.rem(c + d, NC), "row": r}, device_id_type=MESH)
    for dev in (fw, bw, fw_up, bw_dn):
        pl.semaphore_signal(barrier, inc=1, device_id=dev, device_id_type=MESH)
    pl.semaphore_wait(barrier, NR - 1 + NC - 1 + 4)

    def span(row):
        return ext.at[:, pl.ds(pl.multiple_of(HIST + row * SPAN, FL), SPAN)]

    copies = []

    def start(cp):
        cp.start()
        copies.append(cp)

    start(remote(samples.at[row_oth[0]], hop.at[0], s_hop.at[0], r_hop.at[0], fw))
    start(remote(samples.at[row_oth[3]], hop.at[2], s_hop.at[2], r_hop.at[2], bw))
    start(remote(samples.at[row_oth[2]], hop.at[3], s_hop.at[3], r_hop.at[3], bw_dn))
    start(remote(samples.at[row_oth[1]], hop.at[1], s_hop.at[1], r_hop.at[1], fw))
    for d in (2, 1, 3):
        to = row_own[d]
        start(remote(samples.at[to], span(r), s_row.at[d], r_row.at[d], {"chan": c, "row": to}))
    own = pltpu.make_async_copy(samples.at[r], span(r), s_loc.at[0])
    own.start()
    hist = pltpu.make_async_copy(history.at[r], ext.at[:, pl.ds(0, HIST)], s_loc.at[1])
    hist.start()

    def dft_rows(i, _):
        row = i * 16 + lax.broadcasted_iota(jnp.int32, (16, FL), 0)
        q, rest = row // KK, row % KK
        k = (rest // CH) * CHB + q * CH + rest % CH
        n = lax.broadcasted_iota(jnp.int32, (16, FL), 1)
        cv, sv = cos_sin((k * n) & (FL - 1))
        scale = 1.0 / math.sqrt(FL)
        at = pl.ds(pl.multiple_of(i * 16, 16), 16)
        dftc[at, :] = (cv * scale).astype(BF16)
        dfts[at, :] = (-sv * scale).astype(BF16)
        return 0

    lax.fori_loop(0, NCH // 16, dft_rows, 0)

    for k, frm, origin, dev in (
        (0, bw, h_bw * 4 + z, fw),
        (2, fw, h_fw * 4 + z, bw_dn),
        (3, fw_up, h_fw * 4 + zp, bw_dn),
        (1, bw, h_bw * 4 + z, fw_up),
    ):
        remote(hop.at[k], hop.at[k], s_hop.at[k], r_hop.at[k], frm).wait_recv()
        start(remote(hop.at[k], span(origin), s_far.at[k], r_far.at[k], dev))

    def synth_rows(i, _):
        k = i * 16 + lax.broadcasted_iota(jnp.int32, (16, FL), 0)
        n = lax.broadcasted_iota(jnp.int32, (16, FL), 1)
        cv, sv = cos_sin((k * n) & (FL - 1))
        scale = 1.0 / math.sqrt(NCH)
        at = pl.ds(pl.multiple_of(i * 16, 16), 16)
        ptab[at, :] = (cv * scale).astype(BF16)
        qtab[at, :] = (-sv * scale).astype(BF16)
        return 0

    lax.fori_loop(0, NCH // 16, synth_rows, 0)

    for e in range(2):
        for i in range(NC):
            wcos[e * NC + i : e * NC + i + 1, :] = delays[pl.ds(i * 2 * NR + 2 * r + e, 1), :]

    def steer(i, _):
        lanes = pl.ds(pl.multiple_of(i * 128, 128), 128)
        d = wcos[:, lanes]
        cr, ci = cos_sin((d * (c * CHB)) & (FL - 1))
        sr, si = cos_sin(d)
        scale = 1.0 / math.sqrt(A)
        for ch in range(CHB):
            wall[ch, 0:32, lanes] = (cr * scale).astype(BF16)
            wall[ch, 32:64, lanes] = (-ci * scale).astype(BF16)
            cr, ci = cr * sr - ci * si, cr * si + ci * sr
        return 0

    lax.fori_loop(0, A // 128, steer, 0)
    fl[...] = jnp.broadcast_to(flags[pl.ds(r, 1), :].astype(F32), (ROWS, 128)).T

    own.wait()
    hist.wait()
    for d, frm in ((1, row_own[3]), (2, row_own[2]), (3, row_own[1])):
        remote(samples.at[frm], span(frm), s_row.at[d], r_row.at[d], {"chan": c, "row": frm}).wait_recv()
    for k, origin in ((0, row_oth[0]), (1, row_oth[3]), (2, row_oth[1]), (3, row_oth[2])):
        remote(hop.at[k], span(origin), s_far.at[k], r_far.at[k], fw).wait_recv()

    def pfb(i, _):
        lanes = pl.ds(pl.multiple_of(i * 128, 128), 128)
        tap = [jnp.broadcast_to(taps[t : t + 1, lanes], (AL, 128)) for t in range(TAPS)]
        win = [ext[:, pl.ds(pl.multiple_of(t * FL + i * 128, 128), 128)].astype(F32) for t in range(TAPS - 1)]
        for f in range(F):
            win.append(ext[:, pl.ds(pl.multiple_of((f + TAPS - 1) * FL + i * 128, 128), 128)].astype(F32))
            acc = win[f] * tap[0]
            for t in range(1, TAPS):
                acc = acc + win[f + t] * tap[t]
            filt32[f * AL : (f + 1) * AL, :] = acc
        for a in range(AL):
            for b in range(F // 16):
                filt[a * F + b * 16 : a * F + (b + 1) * 16, lanes] = filt32[
                    pl.ds(b * 16 * AL + a, 16, stride=AL), :
                ].astype(BF16)
        return 0

    lax.fori_loop(0, FL // 128, pfb, 0)

    low = lax.broadcasted_iota(jnp.int32, (KK, 128), 1) < 64

    def spectra(q):
        rows = slice(q * KK, (q + 1) * KK)
        re = nt(dftc[rows, :], filt[...])
        im = nt(dfts[rows, :], filt[...])
        for t in range(AL // 2):
            rt = re[:, t * 128 : (t + 1) * 128]
            it = im[:, t * 128 : (t + 1) * 128]
            tmp[(2 * t) * KK : (2 * t + 1) * KK, :] = jnp.where(low, rt, pltpu.roll(it, 64, 1))
            tmp[(2 * t + 1) * KK : (2 * t + 2) * KK, :] = jnp.where(low, pltpu.roll(rt, 64, 1), it)

        def turn(i, _):
            for p in range(CH // 2):
                pair = [tmp[pl.ds(i * CH + 2 * p + e, AL, stride=KK), :] for e in range(2)]
                sbuf[q, i, p * 16 : (p + 1) * 16, :] = jnp.concatenate(pair, axis=0).astype(BF16)
            return 0

        lax.fori_loop(0, NC, turn, 0)
        for d in range(1, NC):
            to = lax.rem(c + d, NC)
            start(remote(sbuf.at[q, to], abuf.at[q, c], s_ch.at[q, d], r_ch.at[q, d], {"chan": to, "row": r}))
        abuf[q, c] = sbuf[q, c]

    def part(row, q, half=None):
        if half is None:
            return g.at[row, pl.ds(q * CH, CH)]
        return g.at[row, pl.ds(q * CH + half * HALF, HALF)]

    def send(q, kind, src, dst, dev):
        start(remote(src, dst, s_g.at[q, kind], r_g.at[q, kind], dev))

    def arrived(q, kind, dst, dev):
        remote(dst, dst, s_g.at[q, kind], r_g.at[q, kind], dev).wait_recv()

    def own_block(q):
        for d in range(1, NC):
            frm = lax.rem(c + NC - d, NC)
            remote(sbuf.at[q, frm], abuf.at[q, frm], s_ch.at[q, d], r_ch.at[q, d], {"chan": frm, "row": r}).wait_recv()
        for p in range(CH // 2):
            x = abuf[q, :, p * 16 : (p + 1) * 16, :].astype(F32)
            for e in range(2):
                v = x[:, e * AL : (e + 1) * AL, :].reshape(ROWS, 128) * fl[...]
                g[r, q * CH + 2 * p + e] = v.astype(BF16)
        send(q, 4, part(r, q, 0), transit.at[0, q], fw)
        send(q, 5, part(r, q, 1), transit.at[1, q], bw)
        send(q, 0, part(r, q), part(r, q), up)
        send(q, 1, part(r, q), part(r, q), dn)

    def cross(q):
        arrived(q, 4, transit.at[0, q], bw)
        send(q, 6, transit.at[0, q], part(h_bw * 4 + z, q, 0), fw)
        arrived(q, 5, transit.at[1, q], fw)
        send(q, 7, transit.at[1, q], part(h_fw * 4 + z, q, 1), bw)

    def relay(q):
        arrived(q, 0, part(row_own[3], q), dn)
        send(q, 2, part(row_own[3], q, 0), part(row_own[3], q, 0), up)
        arrived(q, 1, part(row_own[1], q), up)
        send(q, 3, part(row_own[1], q, 1), part(row_own[1], q, 1), dn)

    def spread(q):
        arrived(q, 6, part(row_oth[0], q, 0), bw)
        send(q, 8, part(row_oth[0], q, 0), part(row_oth[0], q, 0), up)
        send(q, 10, part(row_oth[0], q, 0), part(row_oth[0], q, 0), dn)
        arrived(q, 7, part(row_oth[0], q, 1), fw)
        send(q, 9, part(row_oth[0], q, 1), part(row_oth[0], q, 1), up)
        send(q, 11, part(row_oth[0], q, 1), part(row_oth[0], q, 1), dn)

    def cross2(q):
        arrived(q, 2, part(row_own[2], q, 0), dn)
        send(q, 12, part(row_own[2], q, 0), transit.at[2, q], fw)
        arrived(q, 3, part(row_own[2], q, 1), up)
        send(q, 13, part(row_own[2], q, 1), transit.at[3, q], bw)

    def cross3(q):
        arrived(q, 12, transit.at[2, q], bw)
        send(q, 14, transit.at[2, q], part(h_bw * 4 + z2, q, 0), fw)
        arrived(q, 13, transit.at[3, q], fw)
        send(q, 15, transit.at[3, q], part(h_fw * 4 + z2, q, 1), bw)

    lane = lax.broadcasted_iota(jnp.int32, (32, 128), 1) < 64

    def use(q):
        arrived(q, 8, part(row_oth[3], q, 0), dn)
        arrived(q, 9, part(row_oth[3], q, 1), dn)
        arrived(q, 10, part(row_oth[1], q, 0), up)
        arrived(q, 11, part(row_oth[1], q, 1), up)
        arrived(q, 14, part(row_oth[2], q, 0), bw)
        arrived(q, 15, part(row_oth[2], q, 1), fw)

        def beams(i, _):
            ch = q * CH + i
            acc = jnp.dot(wall[ch], g[:, ch].reshape(A, 128), preferred_element_type=F32)
            turned = pltpu.roll(acc[32:, :], 64, 1)
            bs[pl.ds(pl.multiple_of(i * 32, 32), 32), :] = acc[:32, :] + jnp.where(lane, -turned, turned)
            return 0

        lax.fori_loop(0, CH, beams, 0)

        def pack(i, _):
            pair = [bs[pl.ds(e * 16 + i, CH, stride=32), :] for e in range(2)]
            bsend[q, i] = jnp.concatenate(pair, axis=0).astype(BF16)
            return 0

        lax.fori_loop(0, NC, pack, 0)
        for d in range(1, NC):
            to = lax.rem(c + d, NC)
            start(remote(bsend.at[q, to], z_in.at[q, c], s_bm.at[q, d], r_bm.at[q, d], {"chan": to, "row": r}))
        z_in[q, c] = bsend[q, c]

    def gram_chunk(q):
        def gram(i, _):
            ch = q * CH + i
            acc = nt(gram_lhs(g[r, ch]), g[:, ch].reshape(A, 128))
            vis[ch, 0] = acc[:ROWS].astype(BF16)
            vis[ch, 1] = acc[ROWS:].astype(BF16)
            return 0

        lax.fori_loop(0, CH, gram, 0)

    spectra(0)
    spectra(1)
    spectra(2)
    own_block(0)
    spectra(3)
    own_block(1)
    cross(0)
    own_block(2)
    cross(1)
    relay(0)
    own_block(3)
    cross(2)
    spread(0)
    relay(1)
    cross(3)
    spread(1)
    cross2(0)
    relay(2)
    spread(2)
    cross2(1)
    cross3(0)
    relay(3)
    spread(3)
    cross2(2)
    cross3(1)
    use(0)
    gram_chunk(0)
    cross2(3)
    cross3(2)
    use(1)
    cross3(3)
    gram_chunk(1)
    use(2)
    gram_chunk(2)
    use(3)

    for q in range(Q):
        for d in range(1, NC):
            frm = lax.rem(c + NC - d, NC)
            remote(bsend.at[q, frm], z_in.at[q, frm], s_bm.at[q, d], r_bm.at[q, d], {"chan": frm, "row": r}).wait_recv()
    for cp in copies:
        cp.wait_send()


def front(samples, history, taps, flags, delays):
    vmem = pl.BlockSpec(memory_space=pltpu.VMEM)
    hbm = pl.BlockSpec(memory_space=pl.ANY)
    dma = pltpu.SemaphoreType.DMA
    return pl.pallas_call(
        front_kernel,
        out_shape=(
            pltpu.VMEM((NR, CHB, ROWS, 128), BF16),
            pltpu.VMEM((CHB - CH, 2, ROWS, A), BF16),
            pltpu.VMEM((Q, NC, 2 * CH, 128), BF16),
            pltpu.VMEM((NCH, FL), BF16),
            pltpu.VMEM((NCH, FL), BF16),
        ),
        in_specs=[vmem, hbm, vmem, vmem, vmem],
        out_specs=(vmem,) * 5,
        scratch_shapes=[
            pltpu.VMEM((AL, HIST + F * FL), BF16),
            pltpu.VMEM((4, AL, SPAN), BF16),
            pltpu.VMEM((F * AL, 128), F32),
            pltpu.VMEM((F * AL, FL), BF16),
            pltpu.VMEM((NCH, FL), BF16),
            pltpu.VMEM((NCH, FL), BF16),
            pltpu.VMEM((AL * KK, 128), F32),
            pltpu.VMEM((Q, NC, CH * AL, 128), BF16),
            pltpu.VMEM((Q, NC, CH * AL, 128), BF16),
            pltpu.VMEM((4, Q, HALF, ROWS, 128), BF16),
            pltpu.VMEM((ROWS, 128), F32),
            pltpu.VMEM((32, A), jnp.int32),
            pltpu.VMEM((CHB, 64, A), BF16),
            pltpu.VMEM((CH * 32, 128), F32),
            pltpu.VMEM((Q, NC, 2 * CH, 128), BF16),
            dma((4,)),
            dma((4,)),
            dma((4,)),
            dma((4,)),
            dma((4,)),
            dma((4,)),
            dma((2,)),
            dma((Q, NC)),
            dma((Q, NC)),
            dma((Q, NKIND)),
            dma((Q, NKIND)),
            dma((Q, NC)),
            dma((Q, NC)),
        ],
        compiler_params=pltpu.CompilerParams(
            collective_id=0, has_side_effects=True, vmem_limit_bytes=FRONT_VMEM
        ),
        name="front",
    )(samples, history, taps, flags, delays)


FRONT_VMEM = 40 * 2**20
PARTS = 6


def back_kernel(g, vis, z_in, ptab, qtab, out, series, last, s_vis, s_last):
    r = lax.axis_index("row")
    step = (CHB - CH) // PARTS
    copies = [
        pltpu.make_async_copy(vis.at[pl.ds(i * step, step)], out.at[pl.ds(i * step, step)], s_vis.at[i])
        for i in range(PARTS)
    ]
    for cp in copies:
        cp.start()

    def place(i):
        return pltpu.make_async_copy(last.at[i], out.at[CHB - CH + i], s_last.at[i])

    def gram(i, _):
        ch = CHB - CH + i
        acc = nt(gram_lhs(g[r, ch]), g[:, ch].reshape(A, 128))
        last[i, 0] = acc[:ROWS].astype(BF16)
        last[i, 1] = acc[ROWS:].astype(BF16)
        place(i).start()
        return 0

    lax.fori_loop(0, CH, gram, 0)
    for e in range(2):
        rows = [z_in[q, i].astype(F32)[e * CH : (e + 1) * CH] for i in range(NC) for q in range(Q)]
        zt = jnp.concatenate(rows, axis=0).T.astype(BF16)
        series[e] = jnp.dot(zt[:F, :], ptab[...], preferred_element_type=F32) + jnp.dot(
            zt[F:, :], qtab[...], preferred_element_type=F32
        )
    for cp in copies:
        cp.wait()

    def finish(i, _):
        place(i).wait()
        return 0

    lax.fori_loop(0, CH, finish, 0)


def back(g, vis, z_in, ptab, qtab):
    vmem = pl.BlockSpec(memory_space=pltpu.VMEM)
    return pl.pallas_call(
        back_kernel,
        out_shape=(
            jax.ShapeDtypeStruct((CHB, 2, ROWS, A), BF16),
            jax.ShapeDtypeStruct((2, F, FL), F32),
        ),
        in_specs=[vmem] * 5,
        out_specs=(pl.BlockSpec(memory_space=pl.ANY), vmem),
        scratch_shapes=[
            pltpu.VMEM((CH, 2, ROWS, A), BF16),
            pltpu.SemaphoreType.DMA((PARTS,)),
            pltpu.SemaphoreType.DMA((CH,)),
        ],
        compiler_params=pltpu.CompilerParams(vmem_limit_bytes=BACK_VMEM),
        name="back",
    )(g, vis, z_in, ptab, qtab)


BACK_VMEM = 12 * 2**20


def body(samples, history, antenna_flags, beam_delays):
    held = front(samples, history, jnp.asarray(tap_table()), antenna_flags.reshape(NR, ROWS), beam_delays)
    return back(*held)


def solution(mesh):
    in_specs = (P(None, "chan", "row"), P(None, "chan", None), P(), P())
    out_specs = (P("chan", None, "row", None), P(("chan", "row"), None, None))
    return jax.shard_map(body, mesh=mesh, in_specs=in_specs, out_specs=out_specs, check_vma=False)
```

time: 126 us -> 120 us (0.952)
  Pallas kernels: 123 us -> 119 us
  local copies, waits for them, and re-layouts: 1.79 us -> 0 us
    pallas_call x2, Pallas kernels: 123 us -> 119 us  [the longest x1 112 us: front(): pl.pallas_call(front_kernel, out_shape=(pltpu.VMEM((NR, CHB, ROWS, 128),...]
where the time goes in v1:
time: 120 us
  Pallas kernels  119 us (99%)
    pallas_call x1, Pallas kernels, front(): pl.pallas_call(front_kernel, out_shape=(pltpu.VMEM((NR, CHB, ROWS, 128),...  112 us
    pallas_call x1, Pallas kernels, back(): pl.pallas_call(back_kernel, out_shape=(jax.ShapeDtypeStruct((CHB, 2, ROWS...  6.72 us

profile of v1, /device:TPU:1, one launch (start us, length us, event | category | flops | bytes accessed | tf_op | source)
XLA Modules:
  0.0 119.5 jit_solution(16304000815456681080)
XLA Ops:
  0.6 112.2 %front.1 = (bf16[8,32,128,128]{3,2,1,0:T(8,128)(2,1)S(1)}, bf16[24,2,128,1024]{3,2,1,0:T(8,128)(2,1)S(1)}, bf16[4,16,16,128]{3,2,1,0:T(8,128)(2,1)S(1)}, bf16[51...) custom-call(bf16[8,8,8192]{2,1,0:T(8,128)(2,1)} %samples.1, bf16[8,8,7168]{2,1,0:T(8,128)(2,1)} %history.1, ...), custom_call_target="tpu_custom_call" | custom-call | tf_op jit(solution)/shard_map/front/pallas_call | solution.py:381
  112.8 6.7 %back.1 = (bf16[32,2,128,1024]{3,2,1,0:T(8,128)(2,1)}, f32[2,64,1024]{2,1,0:T(8,128)}) custom-call(bf16[8,32,128,128]{3,2,1,0:T(8,128)(2,1)S(1)} %get-tuple-element.7.g, bf16[24,2,128,1024]{3,2,1,0:T(8,128)(2,1)S(1)} %get-tuple-element.8.vis, bf16[4,16,16,128]{3,2,1,0:T(8,128)(2,1)S(1)} %get-tuple-element.9.z_in, ...), custom_call_target="tpu_custom_call" | custom-call | tf_op jit(solution)/shard_map/back/pallas_call | solution.py:473

commit v2 on v1

--- a/solution.py
+++ b/solution.py
@@ -28,7 +28,7 @@
 MESH = pl.DeviceIdType.MESH
 F32 = jnp.float32
 BF16 = jnp.bfloat16
-NKIND = 16
+NKIND = 11
 
 
 def tap_table():
@@ -66,31 +66,19 @@
 
 def front_kernel(
     samples, history, taps, flags, delays, g, vis, z_in, ptab, qtab,
-    ext, hop, filt32, filt, dftc, dfts, tmp, sbuf, abuf, transit, fl, wcos, wall, bs, bsend,
-    s_row, r_row, s_hop, r_hop, s_far, r_far, s_loc, s_ch, r_ch, s_g, r_g, s_bm, r_bm,
+    ext, dl, filt32, filt, dftc, dfts, tmp, sbuf, abuf, fl, wcos, wall, bs, bsend,
+    s_row, r_row, s_loc, s_ch, r_ch, s_g, r_g, s_bm, r_bm,
 ):
     c = lax.axis_index("chan")
     r = lax.axis_index("row")
-    c_low = lax.rem(c, 8)
-    y_lo = c // 8
     h = r // 4
     z = lax.rem(r, 4)
-    y = 2 * h + y_lo
     zp = lax.rem(z + 1, 4)
     zm = lax.rem(z + 3, 4)
     z2 = lax.rem(z + 2, 4)
-    yp = lax.rem(y + 1, 4)
-    ym = lax.rem(y + 3, 4)
-    h_fw = yp // 2
-    h_bw = ym // 2
-    c_fw = lax.rem(yp, 2) * 8 + c_low
-    c_bw = lax.rem(ym, 2) * 8 + c_low
     up = {"chan": c, "row": h * 4 + zp}
     dn = {"chan": c, "row": h * 4 + zm}
-    fw = {"chan": c_fw, "row": h_fw * 4 + z}
-    bw = {"chan": c_bw, "row": h_bw * 4 + z}
-    fw_up = {"chan": c_fw, "row": h_fw * 4 + zp}
-    bw_dn = {"chan": c_bw, "row": h_bw * 4 + zm}
+    over = {"chan": c, "row": (1 - h) * 4 + z}
     row_own = [h * 4 + v for v in (z, zp, z2, zm)]
     row_oth = [(1 - h) * 4 + v for v in (z, zp, z2, zm)]
 
@@ -104,9 +92,7 @@
         pl.semaphore_signal(barrier, inc=1, device_id={"chan": c, "row": lax.rem(r + d, NR)}, device_id_type=MESH)
     for d in range(1, NC):
         pl.semaphore_signal(barrier, inc=1, device_id={"chan": lax.rem(c + d, NC), "row": r}, device_id_type=MESH)
-    for dev in (fw, bw, fw_up, bw_dn):
-        pl.semaphore_signal(barrier, inc=1, device_id=dev, device_id_type=MESH)
-    pl.semaphore_wait(barrier, NR - 1 + NC - 1 + 4)
+    pl.semaphore_wait(barrier, NR - 1 + NC - 1)
 
     def span(row):
         return ext.at[:, pl.ds(pl.multiple_of(HIST + row * SPAN, FL), SPAN)]
@@ -117,17 +103,15 @@
         cp.start()
         copies.append(cp)
 
-    start(remote(samples.at[row_oth[0]], hop.at[0], s_hop.at[0], r_hop.at[0], fw))
-    start(remote(samples.at[row_oth[3]], hop.at[2], s_hop.at[2], r_hop.at[2], bw))
-    start(remote(samples.at[row_oth[2]], hop.at[3], s_hop.at[3], r_hop.at[3], bw_dn))
-    start(remote(samples.at[row_oth[1]], hop.at[1], s_hop.at[1], r_hop.at[1], fw))
-    for d in (2, 1, 3):
-        to = row_own[d]
+    for d in (6, 7, 5, 2, 4, 1, 3):
+        to = (row_own + row_oth)[d]
         start(remote(samples.at[to], span(r), s_row.at[d], r_row.at[d], {"chan": c, "row": to}))
     own = pltpu.make_async_copy(samples.at[r], span(r), s_loc.at[0])
     own.start()
     hist = pltpu.make_async_copy(history.at[r], ext.at[:, pl.ds(0, HIST)], s_loc.at[1])
     hist.start()
+    late = pltpu.make_async_copy(delays, dl, s_loc.at[2])
+    late.start()
 
     def dft_rows(i, _):
         row = i * 16 + lax.broadcasted_iota(jnp.int32, (16, FL), 0)
@@ -143,15 +127,6 @@
 
     lax.fori_loop(0, NCH // 16, dft_rows, 0)
 
-    for k, frm, origin, dev in (
-        (0, bw, h_bw * 4 + z, fw),
-        (2, fw, h_fw * 4 + z, bw_dn),
-        (3, fw_up, h_fw * 4 + zp, bw_dn),
-        (1, bw, h_bw * 4 + z, fw_up),
-    ):
-        remote(hop.at[k], hop.at[k], s_hop.at[k], r_hop.at[k], frm).wait_recv()
-        start(remote(hop.at[k], span(origin), s_far.at[k], r_far.at[k], dev))
-
     def synth_rows(i, _):
         k = i * 16 + lax.broadcasted_iota(jnp.int32, (16, FL), 0)
         n = lax.broadcasted_iota(jnp.int32, (16, FL), 1)
@@ -164,9 +139,10 @@
 
     lax.fori_loop(0, NCH // 16, synth_rows, 0)
 
+    late.wait()
     for e in range(2):
         for i in range(NC):
-            wcos[e * NC + i : e * NC + i + 1, :] = delays[pl.ds(i * 2 * NR + 2 * r + e, 1), :]
+            wcos[e * NC + i : e * NC + i + 1, :] = dl[pl.ds(i * 2 * NR + 2 * r + e, 1), :]
 
     def steer(i, _):
         lanes = pl.ds(pl.multiple_of(i * 128, 128), 128)
@@ -185,10 +161,11 @@
 
     own.wait()
     hist.wait()
-    for d, frm in ((1, row_own[3]), (2, row_own[2]), (3, row_own[1])):
+    for d, frm in (
+        (1, row_own[3]), (3, row_own[1]), (2, row_own[2]),
+        (4, row_oth[0]), (5, row_oth[3]), (7, row_oth[1]), (6, row_oth[2]),
+    ):
         remote(samples.at[frm], span(frm), s_row.at[d], r_row.at[d], {"chan": c, "row": frm}).wait_recv()
-    for k, origin in ((0, row_oth[0]), (1, row_oth[3]), (2, row_oth[1]), (3, row_oth[2])):
-        remote(hop.at[k], span(origin), s_far.at[k], r_far.at[k], fw).wait_recv()
 
     def pfb(i, _):
         lanes = pl.ds(pl.multiple_of(i * 128, 128), 128)
@@ -253,16 +230,9 @@
             for e in range(2):
                 v = x[:, e * AL : (e + 1) * AL, :].reshape(ROWS, 128) * fl[...]
                 g[r, q * CH + 2 * p + e] = v.astype(BF16)
-        send(q, 4, part(r, q, 0), transit.at[0, q], fw)
-        send(q, 5, part(r, q, 1), transit.at[1, q], bw)
+        send(q, 4, part(r, q), part(r, q), over)
         send(q, 0, part(r, q), part(r, q), up)
         send(q, 1, part(r, q), part(r, q), dn)
-
-    def cross(q):
-        arrived(q, 4, transit.at[0, q], bw)
-        send(q, 6, transit.at[0, q], part(h_bw * 4 + z, q, 0), fw)
-        arrived(q, 5, transit.at[1, q], fw)
-        send(q, 7, transit.at[1, q], part(h_fw * 4 + z, q, 1), bw)
 
     def relay(q):
         arrived(q, 0, part(row_own[3], q), dn)
@@ -270,35 +240,34 @@
         arrived(q, 1, part(row_own[1], q), up)
         send(q, 3, part(row_own[1], q, 1), part(row_own[1], q, 1), dn)
 
+    def relay_tail():
+        q = Q - 1
+        send(q, 9, part(row_own[3], q, 1), part(row_own[3], q, 1), over)
+        send(q, 10, part(row_own[1], q, 1), part(row_own[1], q, 1), over)
+
     def spread(q):
-        arrived(q, 6, part(row_oth[0], q, 0), bw)
-        send(q, 8, part(row_oth[0], q, 0), part(row_oth[0], q, 0), up)
-        send(q, 10, part(row_oth[0], q, 0), part(row_oth[0], q, 0), dn)
-        arrived(q, 7, part(row_oth[0], q, 1), fw)
-        send(q, 9, part(row_oth[0], q, 1), part(row_oth[0], q, 1), up)
-        send(q, 11, part(row_oth[0], q, 1), part(row_oth[0], q, 1), dn)
-
-    def cross2(q):
+        half = 0 if q == Q - 1 else None
+        arrived(q, 4, part(row_oth[0], q), over)
+        send(q, 5, part(row_oth[0], q, half), part(row_oth[0], q, half), up)
+        send(q, 6, part(row_oth[0], q, half), part(row_oth[0], q, half), dn)
+
+    def cross(q):
         arrived(q, 2, part(row_own[2], q, 0), dn)
-        send(q, 12, part(row_own[2], q, 0), transit.at[2, q], fw)
+        send(q, 7, part(row_own[2], q, 0), part(row_own[2], q, 0), over)
         arrived(q, 3, part(row_own[2], q, 1), up)
-        send(q, 13, part(row_own[2], q, 1), transit.at[3, q], bw)
-
-    def cross3(q):
-        arrived(q, 12, transit.at[2, q], bw)
-        send(q, 14, transit.at[2, q], part(h_bw * 4 + z2, q, 0), fw)
-        arrived(q, 13, transit.at[3, q], fw)
-        send(q, 15, transit.at[3, q], part(h_fw * 4 + z2, q, 1), bw)
+        send(q, 8, part(row_own[2], q, 1), part(row_own[2], q, 1), over)
 
     lane = lax.broadcasted_iota(jnp.int32, (32, 128), 1) < 64
 
     def use(q):
-        arrived(q, 8, part(row_oth[3], q, 0), dn)
-        arrived(q, 9, part(row_oth[3], q, 1), dn)
-        arrived(q, 10, part(row_oth[1], q, 0), up)
-        arrived(q, 11, part(row_oth[1], q, 1), up)
-        arrived(q, 14, part(row_oth[2], q, 0), bw)
-        arrived(q, 15, part(row_oth[2], q, 1), fw)
+        half = 0 if q == Q - 1 else None
+        arrived(q, 7, part(row_oth[2], q, 0), over)
+        arrived(q, 8, part(row_oth[2], q, 1), over)
+        if q == Q - 1:
+            arrived(q, 9, part(row_oth[3], q, 1), over)
+            arrived(q, 10, part(row_oth[1], q, 1), over)
+        arrived(q, 5, part(row_oth[3], q, half), dn)
+        arrived(q, 6, part(row_oth[1], q, half), up)
 
         def beams(i, _):
             ch = q * CH + i
@@ -335,36 +304,19 @@
     spectra(2)
     own_block(0)
     spectra(3)
-    own_block(1)
-    cross(0)
-    own_block(2)
-    cross(1)
-    relay(0)
-    own_block(3)
-    cross(2)
-    spread(0)
-    relay(1)
-    cross(3)
-    spread(1)
-    cross2(0)
-    relay(2)
-    spread(2)
-    cross2(1)
-    cross3(0)
-    relay(3)
-    spread(3)
-    cross2(2)
-    cross3(1)
-    use(0)
-    gram_chunk(0)
-    cross2(3)
-    cross3(2)
-    use(1)
-    cross3(3)
-    gram_chunk(1)
-    use(2)
-    gram_chunk(2)
-    use(3)
+    for q in range(1, Q):
+        own_block(q)
+    for q in range(Q):
+        relay(q)
+    relay_tail()
+    for q in range(Q):
+        spread(q)
+    for q in range(Q):
+        cross(q)
+    for q in range(Q):
+        use(q)
+        if q < Q - 1:
+            gram_chunk(q)
 
     for q in range(Q):
         for d in range(1, NC):
@@ -387,11 +339,11 @@
             pltpu.VMEM((NCH, FL), BF16),
             pltpu.VMEM((NCH, FL), BF16),
         ),
-        in_specs=[vmem, hbm, vmem, vmem, vmem],
+        in_specs=[hbm, hbm, vmem, vmem, hbm],
         out_specs=(vmem,) * 5,
         scratch_shapes=[
             pltpu.VMEM((AL, HIST + F * FL), BF16),
-            pltpu.VMEM((4, AL, SPAN), BF16),
+            pltpu.VMEM((BEAMS, A), jnp.int32),
             pltpu.VMEM((F * AL, 128), F32),
             pltpu.VMEM((F * AL, FL), BF16),
             pltpu.VMEM((NCH, FL), BF16),
@@ -399,19 +351,14 @@
             pltpu.VMEM((AL * KK, 128), F32),
             pltpu.VMEM((Q, NC, CH * AL, 128), BF16),
             pltpu.VMEM((Q, NC, CH * AL, 128), BF16),
-            pltpu.VMEM((4, Q, HALF, ROWS, 128), BF16),
             pltpu.VMEM((ROWS, 128), F32),
             pltpu.VMEM((32, A), jnp.int32),
             pltpu.VMEM((CHB, 64, A), BF16),
             pltpu.VMEM((CH * 32, 128), F32),
             pltpu.VMEM((Q, NC, 2 * CH, 128), BF16),
-            dma((4,)),
-            dma((4,)),
-            dma((4,)),
-            dma((4,)),
-            dma((4,)),
-            dma((4,)),
-            dma((2,)),
+            dma((NR,)),
+            dma((NR,)),
+            dma((3,)),
             dma((Q, NC)),
             dma((Q, NC)),
             dma((Q, NKIND)),

time: 120 us -> 110 us (0.917)
  Pallas kernels: 119 us -> 109 us
    pallas_call x1, Pallas kernels: 112 us -> 102 us  [front(): pl.pallas_call(front_kernel, out_shape=(pltpu.VMEM((NR, CHB, ROWS, 128),...]
where the time goes in v2:
time: 110 us
  Pallas kernels  109 us (99%)
    pallas_call x1, Pallas kernels, front(): pl.pallas_call(front_kernel, out_shape=(pltpu.VMEM((NR, CHB, ROWS, 128),...  102 us
    pallas_call x1, Pallas kernels, back(): pl.pallas_call(back_kernel, out_shape=(jax.ShapeDtypeStruct((CHB, 2, ROWS...  6.72 us

profile of v2, /device:TPU:1, one launch (start us, length us, event | category | flops | bytes accessed | tf_op | source)
XLA Modules:
  0.0 109.6 jit_solution(15763410588817699542)
XLA Ops:
  0.6 102.2 %front.1 = (bf16[8,32,128,128]{3,2,1,0:T(8,128)(2,1)S(1)}, bf16[24,2,128,1024]{3,2,1,0:T(8,128)(2,1)S(1)}, bf16[4,16,16,128]{3,2,1,0:T(8,128)(2,1)S(1)}, bf16[51...) custom-call(bf16[8,8,8192]{2,1,0:T(8,128)(2,1)} %samples.1, bf16[8,8,7168]{2,1,0:T(8,128)(2,1)} %history.1, ...), custom_call_target="tpu_custom_call" | custom-call | tf_op jit(solution)/shard_map/front/pallas_call | solution.py:333
  102.9 6.7 %back.1 = (bf16[32,2,128,1024]{3,2,1,0:T(8,128)(2,1)}, f32[2,64,1024]{2,1,0:T(8,128)}) custom-call(bf16[8,32,128,128]{3,2,1,0:T(8,128)(2,1)S(1)} %get-tuple-element.7.g, bf16[24,2,128,1024]{3,2,1,0:T(8,128)(2,1)S(1)} %get-tuple-element.8.vis, bf16[4,16,16,128]{3,2,1,0:T(8,128)(2,1)S(1)} %get-tuple-element.9.z_in, ...), custom_call_target="tpu_custom_call" | custom-call | tf_op jit(solution)/shard_map/back/pallas_call | solution.py:420

commit v3 on v2

v3 whole, which is shorter than its diff:
```python
import math

import jax
import jax.numpy as jnp
import numpy as np
from jax import lax
from jax.experimental import pallas as pl
from jax.experimental.pallas import tpu as pltpu
from jax.sharding import PartitionSpec as P

A = 1024
FL = 1024
NCH = 512
TAPS = 8
BEAMS = 256
NC = 16
NR = 8
CHB = NCH // NC
ROWS = A // NR
AL = ROWS // NC
F = 64
SIZES = (4, 8, 8, 8, 4)
Q = len(SIZES)
OFFS = tuple(sum(SIZES[:q]) for q in range(Q))
BIG = max(SIZES)
HIST = (TAPS - 1) * FL
SPAN = (F // NR) * FL
MESH = pl.DeviceIdType.MESH
F32 = jnp.float32
BF16 = jnp.bfloat16
NKIND = 9


def tap_table():
    position = (np.arange(TAPS * FL, dtype=np.int32).astype(np.float32) + np.float32(0.5)).astype(np.float64)
    centred = position / FL - TAPS / 2.0
    window = 0.5 - 0.5 * np.cos(2.0 * math.pi * position / (TAPS * FL))
    return (np.sinc(centred) * window).reshape(TAPS, FL).astype(np.float32)


def cos_sin(m):
    quarter = lax.shift_right_logical(m, 8)
    x = ((m & 255) - 128).astype(F32) * (2.0 * math.pi / FL)
    x2 = x * x
    s = x * (1.0 + x2 * (-1.0 / 6 + x2 * (1.0 / 120 + x2 * (-1.0 / 5040 + x2 * (1.0 / 362880)))))
    c = 1.0 + x2 * (-0.5 + x2 * (1.0 / 24 + x2 * (-1.0 / 720 + x2 * (1.0 / 40320 + x2 * (-1.0 / 3628800)))))
    root = math.sqrt(0.5)
    ca = (c - s) * root
    sa = (c + s) * root
    odd = (quarter & 1) == 1
    neg = quarter >= 2
    cv = jnp.where(odd, -sa, ca)
    sv = jnp.where(odd, ca, sa)
    return jnp.where(neg, -cv, cv), jnp.where(neg, -sv, sv)


def nt(lhs, rhs):
    return lax.dot_general(lhs, rhs, (((1,), (1,)), ((), ())), preferred_element_type=F32)


def gram_lhs(own):
    low = lax.broadcasted_iota(jnp.int32, (ROWS, 128), 1) < 64
    turned = pltpu.roll(own.astype(F32), 64, 1)
    return jnp.concatenate([own, jnp.where(low, turned, -turned).astype(BF16)], axis=0) * BF16(1.0 / F)


def front_kernel(
    samples, history, taps_in, flags_in, delays, vis, z_in, ptab, qtab,
    g, ext, dl, taps, flags, filt32, filt, dftc, dfts, tmp, sbuf, abuf, fl, wcos, wall, bacc, bs, bsend,
    s_row, r_row, s_loc, s_ch, r_ch, s_g, r_g, s_bm, r_bm,
):
    c = lax.axis_index("chan")
    r = lax.axis_index("row")
    h = r // 4
    z = lax.rem(r, 4)
    zp = lax.rem(z + 1, 4)
    zm = lax.rem(z + 3, 4)
    z2 = lax.rem(z + 2, 4)
    up = {"chan": c, "row": h * 4 + zp}
    dn = {"chan": c, "row": h * 4 + zm}
    over = {"chan": c, "row": (1 - h) * 4 + z}
    row_own = [h * 4 + v for v in (z, zp, z2, zm)]
    row_oth = [(1 - h) * 4 + v for v in (z, zp, z2, zm)]

    def remote(src, dst, ss, rs, dev):
        return pltpu.make_async_remote_copy(
            src_ref=src, dst_ref=dst, send_sem=ss, recv_sem=rs, device_id=dev, device_id_type=MESH
        )

    barrier = pltpu.get_barrier_semaphore()
    for d in range(1, NR):
        pl.semaphore_signal(barrier, inc=1, device_id={"chan": c, "row": lax.rem(r + d, NR)}, device_id_type=MESH)
    for d in range(1, NC):
        pl.semaphore_signal(barrier, inc=1, device_id={"chan": lax.rem(c + d, NC), "row": r}, device_id_type=MESH)

    def span(row):
        return ext.at[:, pl.ds(pl.multiple_of(HIST + row * SPAN, FL), SPAN)]

    local = [
        pltpu.make_async_copy(src, dst, s_loc.at[k])
        for k, (src, dst) in enumerate(
            (
                (samples.at[r], span(r)),
                (history.at[r], ext.at[:, pl.ds(0, HIST)]),
                (delays, dl),
                (taps_in, taps),
                (flags_in, flags),
            )
        )
    ]
    for cp in local:
        cp.start()
    pl.semaphore_wait(barrier, NR - 1 + NC - 1)

    copies = []

    def start(cp):
        cp.start()
        copies.append(cp)

    for d in (6, 7, 5, 2, 4, 1, 3):
        to = (row_own + row_oth)[d]
        start(remote(samples.at[to], span(r), s_row.at[d], r_row.at[d], {"chan": c, "row": to}))
    for q in range(Q):

        def dft_rows(i, _, q=q):
            row = i * 16 + lax.broadcasted_iota(jnp.int32, (16, FL), 0)
            k = (row // SIZES[q]) * CHB + OFFS[q] + row % SIZES[q]
            n = lax.broadcasted_iota(jnp.int32, (16, FL), 1)
            cv, sv = cos_sin((k * n) & (FL - 1))
            scale = 1.0 / math.sqrt(FL)
            at = pl.ds(pl.multiple_of(NC * OFFS[q] + i * 16, 16), 16)
            dftc[at, :] = (cv * scale).astype(BF16)
            dfts[at, :] = (-sv * scale).astype(BF16)
            return 0

        lax.fori_loop(0, SIZES[q], dft_rows, 0)

    def synth_rows(i, _):
        k = i * 16 + lax.broadcasted_iota(jnp.int32, (16, FL), 0)
        n = lax.broadcasted_iota(jnp.int32, (16, FL), 1)
        cv, sv = cos_sin((k * n) & (FL - 1))
        scale = 1.0 / math.sqrt(NCH)
        at = pl.ds(pl.multiple_of(i * 16, 16), 16)
        ptab[at, :] = (cv * scale).astype(BF16)
        qtab[at, :] = (-sv * scale).astype(BF16)
        return 0

    lax.fori_loop(0, NCH // 16, synth_rows, 0)

    local[2].wait()
    local[4].wait()
    for e in range(2):
        for i in range(NC):
            wcos[e * NC + i : e * NC + i + 1, :] = dl[pl.ds(i * 2 * NR + 2 * r + e, 1), :]

    def steer(i, _):
        lanes = pl.ds(pl.multiple_of(i * 128, 128), 128)
        d = wcos[:, lanes]
        cr, ci = cos_sin((d * (c * CHB)) & (FL - 1))
        sr, si = cos_sin(d)
        scale = 1.0 / math.sqrt(A)
        for ch in range(CHB):
            wall[ch, 0:32, lanes] = (cr * scale).astype(BF16)
            wall[ch, 32:64, lanes] = (-ci * scale).astype(BF16)
            cr, ci = cr * sr - ci * si, cr * si + ci * sr
        return 0

    lax.fori_loop(0, A // 128, steer, 0)
    fl[...] = jnp.broadcast_to(flags[pl.ds(r, 1), :].astype(F32), (ROWS, 128)).T

    local[0].wait()
    local[1].wait()
    local[3].wait()
    for d, frm in (
        (1, row_own[3]), (3, row_own[1]), (2, row_own[2]),
        (4, row_oth[0]), (5, row_oth[3]), (7, row_oth[1]), (6, row_oth[2]),
    ):
        remote(samples.at[frm], span(frm), s_row.at[d], r_row.at[d], {"chan": c, "row": frm}).wait_recv()

    def pfb(i, _):
        lanes = pl.ds(pl.multiple_of(i * 128, 128), 128)
        tap = [jnp.broadcast_to(taps[t : t + 1, lanes], (AL, 128)) for t in range(TAPS)]
        win = [ext[:, pl.ds(pl.multiple_of(t * FL + i * 128, 128), 128)].astype(F32) for t in range(TAPS - 1)]
        for f in range(F):
            win.append(ext[:, pl.ds(pl.multiple_of((f + TAPS - 1) * FL + i * 128, 128), 128)].astype(F32))
            acc = win[f] * tap[0]
            for t in range(1, TAPS):
                acc = acc + win[f + t] * tap[t]
            filt32[f * AL : (f + 1) * AL, :] = acc
        for a in range(AL):
            for b in range(F // 16):
                filt[a * F + b * 16 : a * F + (b + 1) * 16, lanes] = filt32[
                    pl.ds(b * 16 * AL + a, 16, stride=AL), :
                ].astype(BF16)
        return 0

    lax.fori_loop(0, FL // 128, pfb, 0)

    def piece(buf, dev, q):
        return buf.at[dev, pl.ds(OFFS[q] * AL, SIZES[q] * AL)]

    def spectra(q):
        size, kk = SIZES[q], NC * SIZES[q]
        low = lax.broadcasted_iota(jnp.int32, (kk, 128), 1) < 64
        rows = slice(NC * OFFS[q], NC * OFFS[q] + kk)
        re = nt(dftc[rows, :], filt[...])
        im = nt(dfts[rows, :], filt[...])
        for t in range(AL // 2):
            rt = re[:, t * 128 : (t + 1) * 128]
            it = im[:, t * 128 : (t + 1) * 128]
            tmp[(2 * t) * kk : (2 * t + 1) * kk, :] = jnp.where(low, rt, pltpu.roll(it, 64, 1))
            tmp[(2 * t + 1) * kk : (2 * t + 2) * kk, :] = jnp.where(low, pltpu.roll(rt, 64, 1), it)

        def turn(i, _):
            for p in range(size // 2):
                pair = [tmp[pl.ds(i * size + 2 * p + e, AL, stride=kk), :] for e in range(2)]
                at = OFFS[q] * AL + p * 16
                sbuf[i, at : at + 16, :] = jnp.concatenate(pair, axis=0).astype(BF16)
            return 0

        lax.fori_loop(0, NC, turn, 0)
        for d in range(1, NC):
            to = lax.rem(c + d, NC)
            start(remote(piece(sbuf, to, q), piece(abuf, c, q), s_ch.at[q, d], r_ch.at[q, d], {"chan": to, "row": r}))
        at = slice(OFFS[q] * AL, (OFFS[q] + size) * AL)
        abuf[c, at, :] = sbuf[c, at, :]

    def part(row, q, half=None):
        if half is None:
            return g.at[row, pl.ds(OFFS[q], SIZES[q])]
        return g.at[row, pl.ds(OFFS[q] + half * (SIZES[q] // 2), SIZES[q] // 2)]

    def send(q, kind, src, dst, dev):
        start(remote(src, dst, s_g.at[q, kind], r_g.at[q, kind], dev))

    def arrived(q, kind, dst, dev):
        remote(dst, dst, s_g.at[q, kind], r_g.at[q, kind], dev).wait_recv()

    def own_block(q):
        for d in range(1, NC):
            frm = lax.rem(c + NC - d, NC)
            remote(piece(sbuf, frm, q), piece(abuf, frm, q), s_ch.at[q, d], r_ch.at[q, d], {"chan": frm, "row": r}).wait_recv()
        for p in range(SIZES[q] // 2):
            at = OFFS[q] * AL + p * 16
            x = abuf[:, at : at + 16, :].astype(F32)
            for e in range(2):
                v = x[:, e * AL : (e + 1) * AL, :].reshape(ROWS, 128) * fl[...]
                g[r, OFFS[q] + 2 * p + e] = v.astype(BF16)
        send(q, 4, part(r, q), part(r, q), over)
        send(q, 0, part(r, q), part(r, q), up)
        send(q, 1, part(r, q), part(r, q), dn)

    def relay(q):
        arrived(q, 0, part(row_own[3], q), dn)
        send(q, 2, part(row_own[3], q, 0), part(row_own[3], q, 0), up)
        arrived(q, 1, part(row_own[1], q), up)
        send(q, 3, part(row_own[1], q, 1), part(row_own[1], q, 1), dn)

    def spread(q):
        arrived(q, 4, part(row_oth[0], q), over)
        send(q, 5, part(row_oth[0], q), part(row_oth[0], q), up)
        send(q, 6, part(row_oth[0], q), part(row_oth[0], q), dn)

    def cross(q):
        arrived(q, 2, part(row_own[2], q, 0), dn)
        send(q, 7, part(row_own[2], q, 0), part(row_own[2], q, 0), over)
        arrived(q, 3, part(row_own[2], q, 1), up)
        send(q, 8, part(row_own[2], q, 1), part(row_own[2], q, 1), over)

    lane = lax.broadcasted_iota(jnp.int32, (32, 128), 1) < 64

    def block(row):
        return pl.ds(pl.multiple_of(row * ROWS, ROWS), ROWS)

    def grams(ch, pair):
        both = jnp.concatenate([g[row, ch] for row in pair], axis=0)
        acc = nt(gram_lhs(g[r, ch]), both).astype(BF16)
        for k, row in enumerate(pair):
            vis[ch, 0, :, block(row)] = acc[:ROWS, k * ROWS : (k + 1) * ROWS]
            vis[ch, 1, :, block(row)] = acc[ROWS:, k * ROWS : (k + 1) * ROWS]

    def beams(ch, pair):
        w = jnp.concatenate([wall[ch, :, block(row)] for row in pair], axis=1)
        x = jnp.concatenate([g[row, ch] for row in pair], axis=0)
        return jnp.dot(w, x, preferred_element_type=F32)

    def own_plane(q):
        def one(i, _):
            ch = OFFS[q] + i
            bacc[ch] = beams(ch, row_own[:2]) + beams(ch, row_own[2:])
            grams(ch, row_own[:2])
            grams(ch, row_own[2:])
            return 0

        lax.fori_loop(0, SIZES[q], one, 0)

    def other_plane(q):
        arrived(q, 7, part(row_oth[2], q, 0), over)
        arrived(q, 8, part(row_oth[2], q, 1), over)

        def one(i, _):
            ch = OFFS[q] + i
            bacc[ch] += beams(ch, row_oth[::2])
            grams(ch, row_oth[::2])
            return 0

        lax.fori_loop(0, SIZES[q], one, 0)

    def last_rows(q):
        arrived(q, 5, part(row_oth[3], q), dn)
        arrived(q, 6, part(row_oth[1], q), up)

        for i in range(SIZES[q]):
            ch = OFFS[q] + i
            acc = bacc[ch] + beams(ch, row_oth[1::2])
            turned = pltpu.roll(acc[32:, :], 64, 1)
            bs[i * 32 : (i + 1) * 32, :] = acc[:32, :] + jnp.where(lane, -turned, turned)

        def leaf(buf, dev):
            return buf.at[dev, pl.ds(2 * OFFS[q], 2 * SIZES[q])]

        for i in range(NC):
            for e in range(2):
                at = 2 * OFFS[q] + e * SIZES[q]
                bsend[i, at : at + SIZES[q], :] = bs[pl.ds(e * 16 + i, SIZES[q], stride=32), :]
        for d in range(1, NC):
            to = lax.rem(c + d, NC)
            start(remote(leaf(bsend, to), leaf(z_in, c), s_bm.at[q, d], r_bm.at[q, d], {"chan": to, "row": r}))
        at = slice(2 * OFFS[q], 2 * (OFFS[q] + SIZES[q]))
        z_in[c, at, :] = bsend[c, at, :]

        def one(i, _):
            grams(OFFS[q] + i, row_oth[1::2])
            return 0

        lax.fori_loop(0, SIZES[q], one, 0)

    spectra(0)
    spectra(1)
    own_block(0)
    spectra(2)
    own_block(1)
    spectra(3)
    spectra(4)
    own_block(2)
    early = len(copies)
    relay(0)
    own_block(3)
    relay(1)
    own_block(4)
    relay(2)
    cross(0)
    relay(3)
    cross(1)
    relay(4)
    for q in range(Q):
        spread(q)
    for cp in copies[:early]:
        cp.wait_send()
    gathered = len(copies)
    for q in range(Q):
        own_plane(q)
        if q + 2 < Q:
            cross(q + 2)
    def collect(q):
        for d in range(1, NC):
            frm = lax.rem(c + NC - d, NC)
            at = pl.ds(2 * OFFS[q], 2 * SIZES[q])
            remote(
                bsend.at[frm, at], z_in.at[frm, at], s_bm.at[q, d], r_bm.at[q, d], {"chan": frm, "row": r}
            ).wait_recv()

    for q in range(Q):
        other_plane(q)
        if q == Q - 1:
            for cp in copies[early:gathered]:
                cp.wait_send()
        last_rows(q)
        if q >= 2:
            collect(q - 2)
    for cp in copies[gathered:]:
        cp.wait_send()
    collect(Q - 2)
    collect(Q - 1)


def front(samples, history, taps, flags, delays):
    vmem = pl.BlockSpec(memory_space=pltpu.VMEM)
    hbm = pl.BlockSpec(memory_space=pl.ANY)
    dma = pltpu.SemaphoreType.DMA
    return pl.pallas_call(
        front_kernel,
        out_shape=(
            pltpu.VMEM((CHB, 2, ROWS, A), BF16),
            pltpu.VMEM((NC, 2 * CHB, 128), F32),
            pltpu.VMEM((NCH, FL), BF16),
            pltpu.VMEM((NCH, FL), BF16),
        ),
        in_specs=[hbm] * 5,
        out_specs=(vmem,) * 4,
        scratch_shapes=[
            pltpu.VMEM((NR, CHB, ROWS, 128), BF16),
            pltpu.VMEM((AL, HIST + F * FL), BF16),
            pltpu.VMEM((BEAMS, A), jnp.int32),
            pltpu.VMEM((TAPS, FL), F32),
            pltpu.VMEM((NR, ROWS), jnp.int32),
            pltpu.VMEM((F * AL, 128), F32),
            pltpu.VMEM((F * AL, FL), BF16),
            pltpu.VMEM((NCH, FL), BF16),
            pltpu.VMEM((NCH, FL), BF16),
            pltpu.VMEM((AL * NC * BIG, 128), F32),
            pltpu.VMEM((NC, CHB * AL, 128), BF16),
            pltpu.VMEM((NC, CHB * AL, 128), BF16),
            pltpu.VMEM((ROWS, 128), F32),
            pltpu.VMEM((32, A), jnp.int32),
            pltpu.VMEM((CHB, 64, A), BF16),
            pltpu.VMEM((CHB, 64, 128), F32),
            pltpu.VMEM((BIG * 32, 128), F32),
            pltpu.VMEM((NC, 2 * CHB, 128), F32),
            dma((NR,)),
            dma((NR,)),
            dma((5,)),
            dma((Q, NC)),
            dma((Q, NC)),
            dma((Q, NKIND)),
            dma((Q, NKIND)),
            dma((Q, NC)),
            dma((Q, NC)),
        ],
        compiler_params=pltpu.CompilerParams(
            collective_id=0, has_side_effects=True, vmem_limit_bytes=FRONT_VMEM
        ),
        name="front",
    )(samples, history, taps, flags, delays)


FRONT_VMEM = 42 * 2**20
PARTS = 16


def back_kernel(vis, z_in, ptab, qtab, out, series_out, series, s_vis, s_ser):
    step = CHB // PARTS
    copies = [
        pltpu.make_async_copy(vis.at[pl.ds(i * step, step)], out.at[pl.ds(i * step, step)], s_vis.at[i])
        for i in range(PARTS)
    ]
    for cp in copies:
        cp.start()
    for e in range(2):
        rows = []
        for i in range(NC):
            for q in range(Q):
                at = 2 * OFFS[q] + e * SIZES[q]
                rows.append(z_in[i, at : at + SIZES[q], :])
        zt = jnp.concatenate(rows, axis=0).T.astype(BF16)
        series[e] = jnp.dot(zt[:F, :], ptab[...], preferred_element_type=F32) + jnp.dot(
            zt[F:, :], qtab[...], preferred_element_type=F32
        )
        cp = pltpu.make_async_copy(series.at[e], series_out.at[e], s_ser.at[e])
        cp.start()
        copies.append(cp)
    for cp in copies:
        cp.wait()


def back(vis, z_in, ptab, qtab):
    vmem = pl.BlockSpec(memory_space=pltpu.VMEM)
    return pl.pallas_call(
        back_kernel,
        out_shape=(
            jax.ShapeDtypeStruct((CHB, 2, ROWS, A), BF16),
            jax.ShapeDtypeStruct((2, F, FL), F32),
        ),
        in_specs=[vmem] * 4,
        out_specs=(pl.BlockSpec(memory_space=pl.ANY),) * 2,
        scratch_shapes=[
            pltpu.VMEM((2, F, FL), F32),
            pltpu.SemaphoreType.DMA((PARTS,)),
            pltpu.SemaphoreType.DMA((2,)),
        ],
        compiler_params=pltpu.CompilerParams(vmem_limit_bytes=BACK_VMEM),
        name="back",
    )(vis, z_in, ptab, qtab)


BACK_VMEM = 8 * 2**20


def body(samples, history, antenna_flags, beam_delays):
    held = front(samples, history, jnp.asarray(tap_table()), antenna_flags.reshape(NR, ROWS), beam_delays)
    return back(*held)


def solution(mesh):
    in_specs = (P(None, "chan", "row"), P(None, "chan", None), P(), P())
    out_specs = (P("chan", None, "row", None), P(("chan", "row"), None, None))
    return jax.shard_map(body, mesh=mesh, in_specs=in_specs, out_specs=out_specs, check_vma=False)
```

time: 110 us -> 108 us (0.982)
  Pallas kernels: 109 us -> 107 us
    pallas_call x1, Pallas kernels: 102 us -> 101 us  [front(): pl.pallas_call(front_kernel, out_shape=(pltpu.VMEM((CHB, 2, ROWS, A), BF1...]
where the time goes in v3:
time: 108 us; the launch traced here: 107 us
  Pallas kernels  107 us (99%)
    pallas_call x1, Pallas kernels, front(): pl.pallas_call(front_kernel, out_shape=(pltpu.VMEM((CHB, 2, ROWS, A), BF1...  101 us
    pallas_call x1, Pallas kernels, back(): pl.pallas_call(back_kernel, out_shape=(jax.ShapeDtypeStruct((CHB, 2, ROWS...  6.11 us

profile of v3, /device:TPU:1, one launch (start us, length us, event | category | flops | bytes accessed | tf_op | source)
XLA Modules:
  0.0 107.5 jit_solution(13638566103151106624)
XLA Ops:
  0.6 100.7 %front.1 = (bf16[32,2,128,1024]{3,2,1,0:T(8,128)(2,1)S(1)}, f32[16,64,128]{2,1,0:T(8,128)S(1)}, bf16[512,1024]{1,0:T(8,128)(2,1)S(1)}, bf16[512,1024]{1,0:T(8,128)(2,1)S(1)}) custom-call(bf16[8,8,8192]{2,1,0:T(8,128)(2,1)} %samples.1, bf16[8,8,7168]{2,1,0:T(8,128)(2,1)} %history.1, f32[8,1024]{1,0:T(8,128)} %constant.2.clone.taps_in, s32[8,128]{1,0:T(8,128)} %bitcast.1, ...), custom_call_target="tpu_custom_call" | custom-call | tf_op jit(solution)/shard_map/front/pallas_call | solution.py:392
  101.4 6.1 %back.1 = (bf16[32,2,128,1024]{3,2,1,0:T(8,128)(2,1)}, f32[2,64,1024]{2,1,0:T(8,128)}) custom-call(bf16[32,2,128,1024]{3,2,1,0:T(8,128)(2,1)S(1)} %get-tuple-element.6.vis, f32[16,64,128]{2,1,0:T(8,128)S(1)} %get-tuple-element.7.z_in, bf16[512,1024]{1,0:T(8,128)(2,1)S(1)} %get-tuple-element.8.ptab, bf16[512,1024]{1,0:T(8,128)(2,1)S(1)} %get-tuple-element.9.qtab), custom_call_target="tpu_custom_call" | custom-call | tf_op jit(solution)/shard_map/back/pallas_call | solution.py:469

commit v4 on v3

--- a/solution.py
+++ b/solution.py
@@ -19,16 +19,18 @@
 ROWS = A // NR
 AL = ROWS // NC
 F = 64
-SIZES = (4, 8, 8, 8, 4)
+SIZES = (4, 8, 8, 4, 8)
 Q = len(SIZES)
 OFFS = tuple(sum(SIZES[:q]) for q in range(Q))
 BIG = max(SIZES)
+SHARED = 4
+SH_OFF = OFFS[SHARED]
 HIST = (TAPS - 1) * FL
 SPAN = (F // NR) * FL
 MESH = pl.DeviceIdType.MESH
 F32 = jnp.float32
 BF16 = jnp.bfloat16
-NKIND = 9
+NKIND = 10
 
 
 def tap_table():
@@ -66,7 +68,7 @@
 
 def front_kernel(
     samples, history, taps_in, flags_in, delays, vis, z_in, ptab, qtab,
-    g, ext, dl, taps, flags, filt32, filt, dftc, dfts, tmp, sbuf, abuf, fl, wcos, wall, bacc, bs, bsend,
+    g, ext, dl, taps, flags, filt32, filt, dft, tmp, sbuf, abuf, fl, wcos, wall, wall2, pout, pin, bacc, bs, bsend,
     s_row, r_row, s_loc, s_ch, r_ch, s_g, r_g, s_bm, r_bm,
 ):
     c = lax.axis_index("chan")
@@ -129,9 +131,9 @@
             n = lax.broadcasted_iota(jnp.int32, (16, FL), 1)
             cv, sv = cos_sin((k * n) & (FL - 1))
             scale = 1.0 / math.sqrt(FL)
-            at = pl.ds(pl.multiple_of(NC * OFFS[q] + i * 16, 16), 16)
-            dftc[at, :] = (cv * scale).astype(BF16)
-            dfts[at, :] = (-sv * scale).astype(BF16)
+            at = 2 * NC * OFFS[q] + i * 16
+            dft[pl.ds(pl.multiple_of(at, 16), 16), :] = (cv * scale).astype(BF16)
+            dft[pl.ds(pl.multiple_of(at + NC * SIZES[q], 16), 16), :] = (-sv * scale).astype(BF16)
             return 0
 
         lax.fori_loop(0, SIZES[q], dft_rows, 0)
@@ -150,23 +152,27 @@
 
     local[2].wait()
     local[4].wait()
-    for e in range(2):
-        for i in range(NC):
-            wcos[e * NC + i : e * NC + i + 1, :] = dl[pl.ds(i * 2 * NR + 2 * r + e, 1), :]
-
-    def steer(i, _):
-        lanes = pl.ds(pl.multiple_of(i * 128, 128), 128)
-        d = wcos[:, lanes]
-        cr, ci = cos_sin((d * (c * CHB)) & (FL - 1))
-        sr, si = cos_sin(d)
-        scale = 1.0 / math.sqrt(A)
-        for ch in range(CHB):
-            wall[ch, 0:32, lanes] = (cr * scale).astype(BF16)
-            wall[ch, 32:64, lanes] = (-ci * scale).astype(BF16)
-            cr, ci = cr * sr - ci * si, cr * si + ci * sr
-        return 0
-
-    lax.fori_loop(0, A // 128, steer, 0)
+    def steer(row, weights, first, lane0, blocks):
+        for e in range(2):
+            for i in range(NC):
+                wcos[e * NC + i : e * NC + i + 1, :] = dl[pl.ds(i * 2 * NR + 2 * row + e, 1), :]
+
+        def one(i, _):
+            d = wcos[:, pl.ds(pl.multiple_of(lane0 + i * 128, 128), 128)]
+            to = pl.ds(pl.multiple_of(i * 128, 128), 128)
+            cr, ci = cos_sin((d * (c * CHB + first)) & (FL - 1))
+            sr, si = cos_sin(d)
+            scale = 1.0 / math.sqrt(A)
+            for ch in range(CHB - first):
+                weights[ch, 0:32, to] = (cr * scale).astype(BF16)
+                weights[ch, 32:64, to] = (-ci * scale).astype(BF16)
+                cr, ci = cr * sr - ci * si, cr * si + ci * sr
+            return 0
+
+        lax.fori_loop(0, blocks, one, 0)
+
+    steer(r, wall, 0, 0, NR)
+    steer(row_oth[0], wall2, SH_OFF, h * (A // 2), NR // 2)
     fl[...] = jnp.broadcast_to(flags[pl.ds(r, 1), :].astype(F32), (ROWS, 128)).T
 
     local[0].wait()
@@ -203,9 +209,8 @@
     def spectra(q):
         size, kk = SIZES[q], NC * SIZES[q]
         low = lax.broadcasted_iota(jnp.int32, (kk, 128), 1) < 64
-        rows = slice(NC * OFFS[q], NC * OFFS[q] + kk)
-        re = nt(dftc[rows, :], filt[...])
-        im = nt(dfts[rows, :], filt[...])
+        both = nt(dft[2 * NC * OFFS[q] : 2 * NC * OFFS[q] + 2 * kk, :], filt[...])
+        re, im = both[:kk], both[kk:]
         for t in range(AL // 2):
             rt = re[:, t * 128 : (t + 1) * 128]
             it = im[:, t * 128 : (t + 1) * 128]
@@ -262,13 +267,26 @@
         send(q, 5, part(row_oth[0], q), part(row_oth[0], q), up)
         send(q, 6, part(row_oth[0], q), part(row_oth[0], q), dn)
 
+    lane = lax.broadcasted_iota(jnp.int32, (32, 128), 1) < 64
+
+    def joined(acc):
+        turned = pltpu.roll(acc[32:, :], 64, 1)
+        return acc[:32, :] + jnp.where(lane, -turned, turned)
+
+    def shared(q, buf):
+        return buf.at[pl.ds(OFFS[q] - SH_OFF, SIZES[q])]
+
     def cross(q):
         arrived(q, 2, part(row_own[2], q, 0), dn)
+        arrived(q, 3, part(row_own[2], q, 1), up)
+        if q >= SHARED:
+            for i in range(SIZES[q]):
+                ch = OFFS[q] + i
+                x = jnp.concatenate([g[h * 4 + v, ch] for v in range(4)], axis=0)
+                pout[ch - SH_OFF] = joined(jnp.dot(wall2[ch - SH_OFF], x, preferred_element_type=F32)).astype(BF16)
+            send(q, 9, shared(q, pout), shared(q, pin), over)
         send(q, 7, part(row_own[2], q, 0), part(row_own[2], q, 0), over)
-        arrived(q, 3, part(row_own[2], q, 1), up)
         send(q, 8, part(row_own[2], q, 1), part(row_own[2], q, 1), over)
-
-    lane = lax.broadcasted_iota(jnp.int32, (32, 128), 1) < 64
 
     def block(row):
         return pl.ds(pl.multiple_of(row * ROWS, ROWS), ROWS)
@@ -301,21 +319,23 @@
 
         def one(i, _):
             ch = OFFS[q] + i
-            bacc[ch] += beams(ch, row_oth[::2])
+            if q < SHARED:
+                bacc[ch] += beams(ch, row_oth[::2])
             grams(ch, row_oth[::2])
             return 0
 
         lax.fori_loop(0, SIZES[q], one, 0)
 
-    def last_rows(q):
-        arrived(q, 5, part(row_oth[3], q), dn)
-        arrived(q, 6, part(row_oth[1], q), up)
-
+    def send_beams(q):
+        if q >= SHARED:
+            arrived(q, 9, shared(q, pin), over)
         for i in range(SIZES[q]):
             ch = OFFS[q] + i
-            acc = bacc[ch] + beams(ch, row_oth[1::2])
-            turned = pltpu.roll(acc[32:, :], 64, 1)
-            bs[i * 32 : (i + 1) * 32, :] = acc[:32, :] + jnp.where(lane, -turned, turned)
+            if q >= SHARED:
+                beam = joined(bacc[ch]) + pin[ch - SH_OFF].astype(F32)
+            else:
+                beam = joined(bacc[ch] + beams(ch, row_oth[1::2]))
+            bs[i * 32 : (i + 1) * 32, :] = beam
 
         def leaf(buf, dev):
             return buf.at[dev, pl.ds(2 * OFFS[q], 2 * SIZES[q])]
@@ -329,6 +349,12 @@
             start(remote(leaf(bsend, to), leaf(z_in, c), s_bm.at[q, d], r_bm.at[q, d], {"chan": to, "row": r}))
         at = slice(2 * OFFS[q], 2 * (OFFS[q] + SIZES[q]))
         z_in[c, at, :] = bsend[c, at, :]
+
+    def last_rows(q):
+        arrived(q, 5, part(row_oth[3], q), dn)
+        arrived(q, 6, part(row_oth[1], q), up)
+        if q < SHARED:
+            send_beams(q)
 
         def one(i, _):
             grams(OFFS[q] + i, row_oth[1::2])
@@ -371,18 +397,22 @@
                 bsend.at[frm, at], z_in.at[frm, at], s_bm.at[q, d], r_bm.at[q, d], {"chan": frm, "row": r}
             ).wait_recv()
 
-    for q in range(Q):
+    for q in range(SHARED):
         other_plane(q)
+        last_rows(q)
+    for q in range(SHARED, Q):
+        send_beams(q)
+        other_plane(q)
+        for k in range(3):
+            collect(k)
         if q == Q - 1:
             for cp in copies[early:gathered]:
                 cp.wait_send()
         last_rows(q)
-        if q >= 2:
-            collect(q - 2)
     for cp in copies[gathered:]:
         cp.wait_send()
-    collect(Q - 2)
-    collect(Q - 1)
+    collect(3)
+    collect(4)
 
 
 def front(samples, history, taps, flags, delays):
@@ -407,14 +437,16 @@
             pltpu.VMEM((NR, ROWS), jnp.int32),
             pltpu.VMEM((F * AL, 128), F32),
             pltpu.VMEM((F * AL, FL), BF16),
-            pltpu.VMEM((NCH, FL), BF16),
-            pltpu.VMEM((NCH, FL), BF16),
+            pltpu.VMEM((2 * NCH, FL), BF16),
             pltpu.VMEM((AL * NC * BIG, 128), F32),
             pltpu.VMEM((NC, CHB * AL, 128), BF16),
             pltpu.VMEM((NC, CHB * AL, 128), BF16),
             pltpu.VMEM((ROWS, 128), F32),
             pltpu.VMEM((32, A), jnp.int32),
             pltpu.VMEM((CHB, 64, A), BF16),
+            pltpu.VMEM((CHB - SH_OFF, 64, A // 2), BF16),
+            pltpu.VMEM((CHB - SH_OFF, 32, 128), BF16),
+            pltpu.VMEM((CHB - SH_OFF, 32, 128), BF16),
             pltpu.VMEM((CHB, 64, 128), F32),
             pltpu.VMEM((BIG * 32, 128), F32),
             pltpu.VMEM((NC, 2 * CHB, 128), F32),

time: 108 us -> 104 us (0.963)
  Pallas kernels: 107 us -> 103 us
    pallas_call x1, Pallas kernels: 101 us -> 96.9 us  [front(): pl.pallas_call(front_kernel, out_shape=(pltpu.VMEM((CHB, 2, ROWS, A), BF1...]
where the time goes in v4:
time: 104 us
  Pallas kernels  103 us (99%)
    pallas_call x1, Pallas kernels, front(): pl.pallas_call(front_kernel, out_shape=(pltpu.VMEM((CHB, 2, ROWS, A), BF1...  96.9 us
    pallas_call x1, Pallas kernels, back(): pl.pallas_call(back_kernel, out_shape=(jax.ShapeDtypeStruct((CHB, 2, ROWS...  6.11 us

profile of v4, /device:TPU:1, one launch (start us, length us, event | category | flops | bytes accessed | tf_op | source)
XLA Modules:
  0.0 103.7 jit_solution(7887602596037539829)
XLA Ops:
  0.6 96.9 %front.1 = (bf16[32,2,128,1024]{3,2,1,0:T(8,128)(2,1)S(1)}, f32[16,64,128]{2,1,0:T(8,128)S(1)}, bf16[512,1024]{1,0:T(8,128)(2,1)S(1)}, bf16[512,1024]{1,0:T(8,128)(2,1)S(1)}) custom-call(bf16[8,8,8192]{2,1,0:T(8,128)(2,1)} %samples.1, bf16[8,8,7168]{2,1,0:T(8,128)(2,1)} %history.1, f32[8,1024]{1,0:T(8,128)} %constant.2.clone.taps_in, s32[8,128]{1,0:T(8,128)} %bitcast.1, ...), custom_call_target="tpu_custom_call" | custom-call | tf_op jit(solution)/shard_map/front/pallas_call | solution.py:422
  97.6 6.1 %back.1 = (bf16[32,2,128,1024]{3,2,1,0:T(8,128)(2,1)}, f32[2,64,1024]{2,1,0:T(8,128)}) custom-call(bf16[32,2,128,1024]{3,2,1,0:T(8,128)(2,1)S(1)} %get-tuple-element.6.vis, f32[16,64,128]{2,1,0:T(8,128)S(1)} %get-tuple-element.7.z_in, bf16[512,1024]{1,0:T(8,128)(2,1)S(1)} %get-tuple-element.8.ptab, bf16[512,1024]{1,0:T(8,128)(2,1)S(1)} %get-tuple-element.9.qtab), custom_call_target="tpu_custom_call" | custom-call | tf_op jit(solution)/shard_map/back/pallas_call | solution.py:501

commit v5 on v4

--- a/solution.py
+++ b/solution.py
@@ -360,7 +360,7 @@
             grams(OFFS[q] + i, row_oth[1::2])
             return 0
 
-        lax.fori_loop(0, SIZES[q], one, 0)
+        lax.fori_loop(0, SIZES[q], one, 0, unroll=q == Q - 1)
 
     spectra(0)
     spectra(1)

time: 104 us -> 104 us (level)
  no operation moved by 1% of the time
where the time goes in v5:
time: 104 us; the launch traced here: 103 us
  Pallas kernels  103 us (99%)
    pallas_call x1, Pallas kernels, front(): pl.pallas_call(front_kernel, out_shape=(pltpu.VMEM((CHB, 2, ROWS, A), BF1...  96.7 us
    pallas_call x1, Pallas kernels, back(): pl.pallas_call(back_kernel, out_shape=(jax.ShapeDtypeStruct((CHB, 2, ROWS...  6.11 us

profile of v5, /device:TPU:1, one launch (start us, length us, event | category | flops | bytes accessed | tf_op | source)
XLA Modules:
  0.0 103.5 jit_solution(1610144642881239910)
XLA Ops:
  0.6 96.7 %front.1 = (bf16[32,2,128,1024]{3,2,1,0:T(8,128)(2,1)S(1)}, f32[16,64,128]{2,1,0:T(8,128)S(1)}, bf16[512,1024]{1,0:T(8,128)(2,1)S(1)}, bf16[512,1024]{1,0:T(8,128)(2,1)S(1)}) custom-call(bf16[8,8,8192]{2,1,0:T(8,128)(2,1)} %samples.1, bf16[8,8,7168]{2,1,0:T(8,128)(2,1)} %history.1, f32[8,1024]{1,0:T(8,128)} %constant.2.clone.taps_in, s32[8,128]{1,0:T(8,128)} %bitcast.1, ...), custom_call_target="tpu_custom_call" | custom-call | tf_op jit(solution)/shard_map/front/pallas_call | solution.py:422
  97.4 6.1 %back.1 = (bf16[32,2,128,1024]{3,2,1,0:T(8,128)(2,1)}, f32[2,64,1024]{2,1,0:T(8,128)}) custom-call(bf16[32,2,128,1024]{3,2,1,0:T(8,128)(2,1)S(1)} %get-tuple-element.6.vis, f32[16,64,128]{2,1,0:T(8,128)S(1)} %get-tuple-element.7.z_in, bf16[512,1024]{1,0:T(8,128)(2,1)S(1)} %get-tuple-element.8.ptab, bf16[512,1024]{1,0:T(8,128)(2,1)S(1)} %get-tuple-element.9.qtab), custom_call_target="tpu_custom_call" | custom-call | tf_op jit(solution)/shard_map/back/pallas_call | solution.py:501
